TPU v7x, 32 devices: a whole 2x2x4 slice. The times are simulated.
32 devices in a mesh: rows: 8 (over z, y), cols: 4 (over x, core).
Axes of the slice: x: 2, y: 2, z: 4, core: 2. Of those that a mesh axis runs over, the one named last changes fastest.
Arguments:
- token_ids: int32 [32, 256], P('rows'), may hold values from 0 to 8191
- keep_mask: int32 [32, 256], P('rows'), may hold values 0 or 1
- remask_order: int32 [8192], P('rows'), may hold values from 0 to 8191, each once
- embed_table: bfloat16 [8192, 1024], P(None, 'cols'), may hold values from -6 to 6
- mask_embed: bfloat16 [1024], P('cols'), may hold values from -4 to 4
- conv_one: bfloat16 [3, 3, 1024, 1024], P(None, None, None, 'cols'), may hold values from -0.0625 to 0.0625
- gain_one: float32 [1024], P('cols'), may hold values from 0.25 to 1.75
- bias_one: float32 [1024], P('cols'), may hold values from -3 to 3
- conv_two: bfloat16 [3, 3, 1024, 1024], P(None, None, None, 'cols'), may hold values from -0.0625 to 0.0625
- gain_two: float32 [1024], P('cols'), may hold values from 0.25 to 1.75
- bias_two: float32 [1024], P('cols'), may hold values from -3 to 3
- head_weight: bfloat16 [1024, 8192], P(None, 'cols'), may hold values from -15.6 to 15.6
Outputs:
- features: bfloat16 [32, 256, 1024], P('rows', None, 'cols')
- token_logp: float32 [32, 256], P('rows', 'cols')
Inputs may be any that keep to these rules, and one draw needn't show every extreme that they name: `remask_order`: each rank appears once.
All inputs are finite; a program needn't handle non-finite values. No bound on the sum of `keep_mask` on one device may be relied on, other than what follows from the above.
Results may differ from a plain program's by a relative error of at most 0.0039.
Values may be sent and summed in bfloat16 or wider, within the bound.
No kernel may reach another device: no remote copies, remote signals or barrier semaphores. Data moves between devices by JAX's collectives and lax.ppermute only.
A program may use at most 128 MiB of HBM per device.

v0:
```python
import jax
import jax.numpy as jnp
from jax import lax
from jax.experimental import pallas as pl
from jax.experimental.pallas import tpu as pltpu
from jax.sharding import PartitionSpec as P


GROUPS = 32
EPS = 1e-05
PAD = 16
F32 = jnp.float32
BF16 = jnp.bfloat16
VMEM = pl.BlockSpec(memory_space=pltpu.VMEM)
SMEM = pl.BlockSpec(memory_space=pltpu.SMEM)
HBM = pl.BlockSpec(memory_space=pltpu.HBM)


def swap(value):
    n = lax.axis_size("cols")
    return lax.ppermute(value, "cols", [(i, i ^ 1) for i in range(n)])


def cross(value):
    n = lax.axis_size("cols")
    return [
        lax.ppermute(value, "cols", [(i, (i + 2 * s) % n) for i in range(n)])
        for s in range(1, n // 2)
    ]


def sources():
    n = lax.axis_size("cols")
    me = lax.axis_index("cols")
    out = []
    for s in range(n // 2):
        same = lax.rem(me + n - 2 * s, n)
        out += [same, same ^ 1]
    return out


def gathered(value, after=None):
    out = [value, swap(value)]
    for far in cross(value):
        if after is not None:
            far, _ = lax.optimization_barrier((far, after))
        out += [far, swap(far)]
    return out


def far_blocks(values, after):
    out = []
    for far in values:
        far, _ = lax.optimization_barrier((far, after))
        out += [far, swap(far)]
    return out


def upward(value):
    n = lax.axis_size("rows")
    return lax.ppermute(value, "rows", [(i, i + 1) for i in range(n - 1)])


def downward(value):
    n = lax.axis_size("rows")
    return lax.ppermute(value, "rows", [(i + 1, i) for i in range(n - 1)])


def tile_sum(value):
    return jnp.sum(value, axis=0, keepdims=True)


def load_taps(src, first, w, held, sems):
    here = w.shape[3]
    copies = []
    for b in range(3):
        for k in range(held.shape[0]):
            at = pl.multiple_of(src[first + k] * here, here)
            copy = pltpu.make_async_copy(
                w.at[:, b, pl.ds(at, here), :], held.at[k, b], sems.at[b, k]
            )
            copy.start()
            copies.append(copy)
    return copies


def taps(fields, held, b, i, total):
    for k, field in enumerate(fields):
        for a in range(3):
            part = jnp.dot(field(a + i), held[k, b, a], preferred_element_type=F32)
            total = part if total is None else total + part
    return total


def joined_taps(before, here, after):
    width = here.shape[0]
    col = lax.broadcasted_iota(jnp.int32, here.shape, 0)
    left = jnp.where(col == 0, 0.0, pltpu.roll(before, 1, 0))
    right = jnp.where(col == width - 1, 0.0, pltpu.roll(after, width - 1, 0))
    return here + left + right


def finish(parts, y_ref, packed_ref, stats_ref, rows, width, per_group):
    here = y_ref.shape[1]
    count = rows * width
    total = jnp.zeros((1, here), F32)
    for i in range(rows):
        y = joined_taps(parts[0, i], parts[1, i], parts[2, i])
        y_ref[i * width : (i + 1) * width, :] = y
        total = total + tile_sum(y)
    mean = total / count
    centre = mean.astype(BF16).astype(F32)
    square = jnp.zeros((1, here), F32)
    for i in range(rows):
        dev = y_ref[i * width : (i + 1) * width, :] - centre
        packed_ref[i * width : (i + 1) * width, :] = dev.astype(BF16)
        square = square + tile_sum(dev * dev)
    packed_ref[count : count + PAD, :] = jnp.broadcast_to(centre, (PAD, here)).astype(BF16)
    spread = square - count * (mean - centre) * (mean - centre)
    same = (
        lax.broadcasted_iota(jnp.int32, (here, here), 0) // per_group
        == lax.broadcasted_iota(jnp.int32, (here, here), 1) // per_group
    ).astype(F32)

    def over_group(value):
        return jnp.dot(
            jnp.broadcast_to(value, (8, here)),
            same,
            precision=lax.Precision.HIGHEST,
            preferred_element_type=F32,
        )

    mid = over_group(mean) / per_group
    away = mean - mid[:1]
    stats_ref[0] = mid
    stats_ref[1] = over_group(spread + count * away * away)


def reader(rows, width, main, inner, outer=None):
    def read(r):
        if r == 0:
            return outer[0:width, :]
        if r == 1:
            return inner[0:width, :]
        if r == rows + 2:
            return inner[width : 2 * width, :]
        if r == rows + 3:
            return outer[width : 2 * width, :]
        return main[(r - 2) * width : (r - 1) * width, :]

    return read


def conv_near(rows, width, src, *refs):
    fields, (w, parts, far, held, sems, far_sems) = refs[:6], refs[6:]
    copies = load_taps(src, 0, w, held, sems)
    later = load_taps(src, 2, w, far, far_sems)
    readers = [reader(rows, width, *fields[3 * k : 3 * k + 3]) for k in range(2)]
    for b in range(3):
        for copy in copies[2 * b : 2 * b + 2]:
            copy.wait()
        for i in range(rows + 2):
            parts[b, i] = taps(readers, held, b, i, None)
    for copy in later:
        copy.wait()


def fetch_taps(src, w, held, sems):
    for copy in load_taps(src, 0, w, held, sems):
        copy.wait()


def fetch_head(src, w, held, sems):
    n, here = held.shape[0], held.shape[1]
    copies = []
    for k in range(n):
        at = pl.multiple_of(src[k] * here, here)
        copies.append(pltpu.make_async_copy(w.at[pl.ds(at, here), :], held.at[k], sems.at[k]))
        copies[-1].start()
    for copy in copies:
        copy.wait()


def conv_far(rows, width, per_group, *refs):
    fields, (held, before, packed, stats, parts, y) = refs[:-6], refs[-6:]
    readers = [reader(rows, width, *fields[k : k + 2]) for k in range(0, len(fields), 2)]
    for b in range(3):
        for i in range(rows):
            parts[b, i] = taps(readers, held, b, i + 1, before[b, i + 1])
    finish(parts, y, packed, stats, rows, width, per_group)


def conv_edge(rows, width, *refs):
    fields, (held, before, packed, out) = refs[:-4], refs[-4:]
    readers = [reader(rows, width, *fields[k : k + 3]) for k in range(0, len(fields), 3)]
    count = rows * width
    centre = packed[count : count + PAD, :].astype(F32)[:1]
    for j, i in enumerate((0, rows + 1)):
        y = joined_taps(*[taps(readers, held, b, i, before[b, i]) for b in range(3)])
        out[j * width : (j + 1) * width, :] = (y - centre).astype(BF16)


def activated(rows, width, flags, fields, norms, hidden):
    count = rows * width
    for k in range(len(norms)):
        main, edge = fields[2 * k : 2 * k + 2]
        scale = norms[k][0][:1]
        mid = main[count : count + PAD, :].astype(F32)[:1]
        shift = mid * scale + norms[k][1][:1]
        for r in range(rows + 2):
            if r == 0:
                v = edge[0:width, :]
            elif r == rows + 1:
                v = edge[width : 2 * width, :]
            else:
                v = main[(r - 1) * width : r * width, :]
            v = v.astype(F32) * scale + shift
            v = v * (0.5 + 0.5 * jnp.tanh(0.5 * v))
            if r == 0:
                v = jnp.where(flags[0] > 0, v, 0.0)
            if r == rows + 1:
                v = jnp.where(flags[1] > 0, v, 0.0)
            hidden[k, r * width : (r + 1) * width, :] = v.astype(BF16)
    return [
        (lambda r, k=k: hidden[k, r * width : (r + 1) * width, :]) for k in range(len(norms))
    ]


def second_near(rows, width, flags, *refs):
    fields, norms, (held, parts, hidden) = refs[:4], refs[4:6], refs[6:]
    readers = activated(rows, width, flags, fields, norms, hidden)
    for b in range(3):
        for i in range(rows):
            parts[b, i] = taps(readers, held, b, i, None)


def second_far(rows, width, per_group, n, flags, *refs):
    fields, norms = refs[: 2 * n], refs[2 * n : 3 * n]
    held, near, y, packed, stats, parts, hidden = refs[3 * n :]
    held = held.at[2:]
    readers = activated(rows, width, flags, fields, norms, hidden)
    for b in range(3):
        for i in range(rows):
            parts[b, i] = taps(readers, held, b, i, near[b, i])
    finish(parts, y, packed, stats, rows, width, per_group)


def head(count, n, tile, *refs):
    starts, devs, norms = refs[:n], refs[n : 2 * n], refs[2 * n : 3 * n]
    held, ids, out, feat, logits, top, summed, picked = refs[3 * n :]
    step = 256
    tiles = held.shape[2] // tile
    for k in range(n):
        scale = norms[k][0][:1]
        mid = devs[k][count : count + PAD, :].astype(F32)[:1]
        shift = mid * scale + norms[k][1][:1]
        for r in range(0, count, step):
            value = devs[k][r : r + step, :].astype(F32) * scale + shift
            feat[k, r : r + step, :] = (starts[k][r : r + step, :].astype(F32) + value).astype(BF16)
    top[...] = jnp.full(top.shape, -jnp.inf, F32)
    summed[...] = jnp.zeros(summed.shape, F32)
    picked[...] = jnp.zeros(picked.shape, F32)

    def multiply(t, slot):
        total = None
        for k in range(n):
            part = jnp.dot(
                feat[k],
                held[k, :, pl.ds(pl.multiple_of(t * tile, tile), tile)],
                preferred_element_type=F32,
            )
            total = part if total is None else total + part
        logits[slot] = total

    def reduce(t, slot):
        for r in range(0, count, 64):
            rows = slice(r, r + 64)
            pieces = [logits[slot, rows, g : g + 128] for g in range(0, tile, 128)]
            old = top[rows, :]
            new = old
            for piece in pieces:
                new = jnp.maximum(new, piece)
            total = summed[rows, :] * jnp.exp(old - new)
            hit = picked[rows, :]
            rel = ids[rows, :] - t * tile
            for g, piece in enumerate(pieces):
                total = total + jnp.exp(piece - new)
                hit = jnp.where(rel == g * 128, piece, hit)
            top[rows, :] = new
            summed[rows, :] = total
            picked[rows, :] = hit

    multiply(0, 0)

    def body(t, carry):
        multiply(t, lax.rem(t, 2))
        reduce(t - 1, lax.rem(t + 1, 2))
        return carry

    lax.fori_loop(1, tiles, body, 0)
    reduce(tiles - 1, (tiles - 1) % 2)
    lane = lax.broadcasted_iota(jnp.int32, (128, 128), 1)
    for r in range(0, count, 128):
        rows = slice(r, r + 128)
        high = jnp.max(top[rows, :], axis=1, keepdims=True)
        total = jnp.sum(summed[rows, :] * jnp.exp(top[rows, :] - high), axis=1, keepdims=True)
        hit = jnp.sum(picked[rows, :], axis=1, keepdims=True)
        stacked = jnp.where(lane == 0, high, jnp.where(lane == 1, total, hit))
        out[:, rows] = jnp.transpose(stacked)[:8]


def in_hbm(value):
    return pltpu.with_memory_space_constraint(value, pltpu.HBM)


def params(mib):
    return pltpu.CompilerParams(vmem_limit_bytes=mib << 20)


def over_rows(stats, count, per_group, gains, biases, between=None):
    stats = jnp.stack([stats] + cross(stats))
    population = float(count * per_group)
    n = lax.axis_size("rows")
    step = 1
    while step < n:
        radix = 4 if step > 1 and n // step % 4 == 0 else 2
        others = []
        for j in range(1, radix):
            move = [(i, i ^ (step * j)) for i in range(n)]
            others.append(lax.ppermute(stats, "rows", move))
        states = [stats] + others
        mid = sum(t[:, 0] for t in states) / radix
        away = sum((t[:, 0] - mid) * (t[:, 0] - mid) for t in states)
        stats = jnp.stack([mid, sum(t[:, 1] for t in states) + population * away], axis=1)
        population *= radix
        step *= radix
        if between is not None:
            between(stats)
            between = None
    scale = gains / jnp.sqrt(stats[:, 1] / population + EPS)
    mine = jnp.stack([scale, biases - stats[:, 0] * scale], axis=1)
    other = swap(mine)
    return [f for k in range(mine.shape[0]) for f in (mine[k], other[k])]


def step_of(
    token_ids,
    keep_mask,
    remask_order,
    embed_table,
    mask_embed,
    conv_one,
    gain_one,
    bias_one,
    conv_two,
    gain_two,
    bias_two,
    head_weight,
):
    rows, width = token_ids.shape
    n_rows = lax.axis_size("rows")
    n = lax.axis_size("cols")
    height = rows * n_rows
    here = gain_one.shape[0]
    per_group = here * n // GROUPS
    count = rows * width
    me_row = lax.axis_index("rows")
    flags = jnp.stack([me_row > 0, me_row < n_rows - 1]).astype(jnp.int32)
    src = jnp.stack(sources()).astype(jnp.int32)

    def look(codes):
        rows_of = jnp.take(embed_table, jnp.maximum(codes - 2, 0), axis=0, mode="clip")
        rows_of = jnp.where(codes[:, None] == 1, mask_embed[None, :], rows_of)
        return jnp.where(codes[:, None] == 0, 0, rows_of)

    looked = jnp.take(embed_table, token_ids.reshape(-1), axis=0, mode="clip")
    main_far = cross(looked)
    token_ids, keep_mask, remask_order, looked = lax.optimization_barrier(
        (token_ids, keep_mask, remask_order, looked)
    )
    visible = (keep_mask.reshape(-1) == 1) | (remask_order >= height * width // 2)
    code = jnp.where(visible, token_ids.reshape(-1) + 2, 1)
    start = jnp.where(visible[:, None], looked, mask_embed[None, :])
    above, below = upward(code[count - 2 * width :]), downward(code[: 2 * width])
    halo = look(
        jnp.concatenate([above[width:], below[:width], above[:width], below[width:]])
    )
    inner, outer = halo[: 2 * width], halo[2 * width :]
    mains = [start, swap(start)]
    inners, inner_far = [inner, swap(inner)], cross(inner)
    outers, outer_far = [outer, swap(outer)], cross(outer)

    packed_shape = jax.ShapeDtypeStruct((count + PAD, here), BF16)
    stats_shape = jax.ShapeDtypeStruct((2, 8, here), F32)
    parts_shape = (3, rows, width, here)
    y_shape = (count, here)
    own = jnp.stack([gain_one, bias_one, gain_two, bias_two, mask_embed.astype(F32)])
    own = jnp.broadcast_to(own[:, None], (5, 8, here))
    affine = jnp.stack([own] + cross(own))
    mask_far = affine[1:, 4, 0].astype(BF16)
    main_far = [
        jnp.where(visible[:, None], far, mask_far[k]) for k, far in enumerate(main_far)
    ]
    fields = [f for k in range(2) for f in (mains[k], inners[k], outers[k])]
    vocab_here = head_weight.shape[1]
    near, taps_far = pl.pallas_call(
        lambda *refs: conv_near(rows, width, *refs),
        out_shape=(
            jax.ShapeDtypeStruct((3, rows + 2, width, here), F32),
            jax.ShapeDtypeStruct((n - 2, 3, 3, here, here), BF16),
        ),
        in_specs=[SMEM] + [VMEM] * 6 + [HBM],
        out_specs=(VMEM,) * 2,
        scratch_shapes=[
            pltpu.VMEM((2, 3, 3, here, here), BF16),
            pltpu.SemaphoreType.DMA((3, 2)),
            pltpu.SemaphoreType.DMA((3, n - 2)),
        ],
        compiler_params=params(12),
        name="conv_near",
    )(src, *fields, in_hbm(conv_one))
    mains += far_blocks(main_far, near)
    inners += far_blocks(inner_far, near)
    outers += far_blocks(outer_far, near)
    fields = [f for k in range(2, n) for f in (mains[k], inners[k])]
    packed, stats = pl.pallas_call(
        lambda *refs: conv_far(rows, width, per_group, *refs),
        out_shape=(packed_shape, stats_shape),
        in_specs=[VMEM] * (len(fields) + 2),
        out_specs=(VMEM, VMEM),
        scratch_shapes=[pltpu.VMEM(parts_shape, F32), pltpu.VMEM(y_shape, F32)],
        compiler_params=params(12),
        name="conv_far",
    )(*fields, taps_far, near)
    fields = [f for k in range(2, n) for f in (mains[k], inners[k], outers[k])]
    edge_box = []

    def make_edge(state):
        centre, _ = lax.optimization_barrier((packed, state))
        edge_box.append(
            pl.pallas_call(
                lambda *refs: conv_edge(rows, width, *refs),
                out_shape=jax.ShapeDtypeStruct((2 * width, here), BF16),
                in_specs=[VMEM] * (len(fields) + 3),
                out_specs=VMEM,
                compiler_params=params(8),
                name="conv_edge",
            )(*fields, taps_far, near, centre)
        )

    norms = over_rows(stats, count, per_group, affine[:, 0], affine[:, 1], make_edge)
    blocks = gathered(packed, norms[0])
    edges = gathered(edge_box[0], norms[0])
    fields = [f for two in zip(blocks, edges) for f in two]
    when, _ = lax.optimization_barrier((src, edge_box[0]))
    taps_two = pl.pallas_call(
        fetch_taps,
        out_shape=jax.ShapeDtypeStruct((n, 3, 3, here, here), BF16),
        in_specs=[SMEM, HBM],
        out_specs=VMEM,
        scratch_shapes=[pltpu.SemaphoreType.DMA((3, n))],
        compiler_params=params(8),
        name="fetch_two",
    )(when, in_hbm(conv_two))
    near = pl.pallas_call(
        lambda *refs: second_near(rows, width, *refs),
        out_shape=jax.ShapeDtypeStruct(parts_shape, F32),
        in_specs=[SMEM] + [VMEM] * 7,
        out_specs=VMEM,
        scratch_shapes=[pltpu.VMEM((2, count + 2 * width, here), BF16)],
        compiler_params=params(12),
        name="two_near",
    )(flags, *fields[:4], *norms[:2], taps_two)
    fields = fields[:4] + list(
        lax.optimization_barrier((near, *fields[4:]))
    )
    near = fields.pop(4)
    y_two, packed, stats = pl.pallas_call(
        lambda *refs: second_far(rows, width, per_group, n - 2, *refs),
        out_shape=(jax.ShapeDtypeStruct(y_shape, F32), packed_shape, stats_shape),
        in_specs=[SMEM] + [VMEM] * (3 * (n - 2) + 2),
        out_specs=(VMEM, VMEM, VMEM),
        scratch_shapes=[
            pltpu.VMEM(parts_shape, F32),
            pltpu.VMEM((n - 2, count + 2 * width, here), BF16),
        ],
        compiler_params=params(12),
        name="two_far",
    )(flags, *fields[4:], *norms[2:], taps_two, near)

    norms = over_rows(stats, count, per_group, affine[:, 2], affine[:, 3])
    blocks = gathered(packed, norms[0])
    when, _ = lax.optimization_barrier((src, packed))
    head_in = pl.pallas_call(
        fetch_head,
        out_shape=jax.ShapeDtypeStruct((n, here, vocab_here), BF16),
        in_specs=[SMEM, HBM],
        out_specs=VMEM,
        scratch_shapes=[pltpu.SemaphoreType.DMA((n,))],
        compiler_params=params(8),
        name="fetch_head",
    )(when, in_hbm(head_weight))
    features = start.astype(F32) + (y_two * norms[0][0, :1] + norms[0][1, :1])
    features = features.astype(BF16).reshape(rows, width, here)

    ids = token_ids.reshape(-1, 1) - lax.axis_index("cols") * vocab_here
    ids = ids - lax.broadcasted_iota(jnp.int32, (1, 128), 1)
    tile = min(512, vocab_here)
    state = pl.pallas_call(
        lambda *refs: head(count, n, tile, *refs),
        out_shape=jax.ShapeDtypeStruct((8, count), F32),
        in_specs=[VMEM] * (3 * n + 2),
        out_specs=VMEM,
        scratch_shapes=[
            pltpu.VMEM((n, count, here), BF16),
            pltpu.VMEM((2, count, tile), F32),
            pltpu.VMEM((count, 128), F32),
            pltpu.VMEM((count, 128), F32),
            pltpu.VMEM((count, 128), F32),
        ],
        compiler_params=params(16),
        name="head",
    )(*mains, *blocks, *norms, head_in, ids)
    step = 1
    while step < n:
        other = lax.ppermute(state, "cols", [(i, i ^ step) for i in range(n)])
        high = jnp.maximum(state[0], other[0])
        total = state[1] * jnp.exp(state[0] - high) + other[1] * jnp.exp(other[0] - high)
        state = jnp.stack([high, total, state[2] + other[2]])
        step *= 2
    logp = (state[2] - state[0] - jnp.log(state[1])).reshape(rows, width)
    slice_width = width // n
    token_logp = lax.dynamic_slice_in_dim(
        logp, lax.axis_index("cols") * slice_width, slice_width, 1
    )
    return (features, token_logp)


def solution(mesh):
    in_specs = (
        P("rows", None),
        P("rows", None),
        P("rows"),
        P(None, "cols"),
        P("cols"),
        P(None, None, None, "cols"),
        P("cols"),
        P("cols"),
        P(None, None, None, "cols"),
        P("cols"),
        P("cols"),
        P(None, "cols"),
    )
    out_specs = (P("rows", None, "cols"), P("rows", "cols"))
    return jax.shard_map(step_of, mesh=mesh, in_specs=in_specs, out_specs=out_specs, check_vma=False)
```

profile of v0, /device:TPU:0, one launch (start us, length us, event | category | flops | bytes accessed | tf_op | source)
XLA Modules:
  0.0 115.7 jit_solution(9616222874825521725)
XLA Ops:
  1.5 6.2 %gather_fusion = bf16[1024,256]{1,0:T(8,128)(2,1)S(1)} fusion(bf16[8192,256]{1,0:T(8,128)(2,1)} %param.15, s32[1024]{0:T(1024)S(1)} %broadcast_clamp_fusion.1), kind=kCustom, calls=%fused_computation | custom fusion | bytes 1052672 | tf_op jit(solution)/shard_map/jit(_take)/gather | solution.py:376
  7.8 1.3 %collective-permute-start.3 = (s32[512]{0:T(512)S(1)}, s32[512]{0:T(512)S(1)}, u32[]{:S(2)}, u32[]{:S(2)}) collective-permute-start(s32[512]{0:T(512)S(1)} %get-tuple-element.98), channel_id=1, source_target_pairs={{4,0},{8,4},{12,8},{16,12},{20,16},{24,20},{28,24},{5,1},{9,5},{13... | collective-permute-start | bytes 6152 | tf_op jit(solution)/shard_map/ppermute | solution.py:66
  9.1 3.0 %collective-permute-start = (bf16[1024,256]{1,0:T(8,128)(2,1)S(1)}, bf16[1024,256]{1,0:T(8,128)(2,1)S(1)}, u32[]{:S(2)}, u32[]{:S(2)}) collective-permute-start(bf16[1024,256]{1,0:T(8,128)(2,1)S(1)} %gather_fusion), channel_id=1, source_target_pairs={{0,2},{1,3},{2,0},{3,1},{4,6},{5,7},{6,4},{7,5},{8,10},{9,11},{10,... | collective-permute-start | bytes 1572872 | tf_op jit(solution)/shard_map/ppermute | solution.py:27
  12.3 4.5 %collective-permute-start.2 = (s32[512]{0:T(512)S(1)}, s32[512]{0:T(512)S(1)}, u32[]{:S(2)}, u32[]{:S(2)}) collective-permute-start(s32[512]{0:T(512)S(1)} %get-tuple-element.97), channel_id=1, source_target_pairs={{0,4},{4,8},{8,12},{12,16},{16,20},{20,24},{24,28},{1,5},{5,9},{9,... | collective-permute-start | bytes 6152 | tf_op jit(solution)/shard_map/ppermute | solution.py:61
  16.8 1.3 %collective-permute-done.2 = s32[512]{0:T(512)S(1)} collective-permute-done((s32[512]{0:T(512)S(1)}, s32[512]{0:T(512)S(1)}, u32[]{:S(2)}, u32[]{:S(2)}) %collective-permute-start.2) | collective-permute-done | bytes 2080 | tf_op jit(solution)/shard_map/ppermute | solution.py:61
  18.1 6.2 %gather_fusion.1 = bf16[1024,256]{1,0:T(8,128)(2,1)S(1)} fusion(bf16[8192,256]{1,0:T(8,128)(2,1)} %param.15, s32[1024]{0:T(1024)S(1)} %broadcast_clamp_fusion), kind=kCustom, calls=%fused_computation.1 | custom fusion | bytes 1052672 | tf_op jit(solution)/shard_map/jit(_take)/gather | solution.py:372
  26.8 1.7 %collective-permute-start.7 = (bf16[512,256]{1,0:T(8,128)(2,1)S(1)}, bf16[512,256]{1,0:T(8,128)(2,1)S(1)}, u32[]{:S(2)}, u32[]{:S(2)}) collective-permute-start(bf16[512,256]{1,0:T(8,128)(2,1)S(1)} %get-tuple-element.74.refs_2_), channel_id=1, source_target_pairs={{0,2},{1,3},{2,0},{3,1},{4,6},{5,7},{6,4},{7,5},{8,10},{9,11},{10,... | collective-permute-start | bytes 786440 | tf_op jit(solution)/shard_map/ppermute | solution.py:27
  28.7 6.1 %conv_near.1 = (f32[3,6,256,256]{3,2,1,0:T(8,128)S(1)}, bf16[2,3,3,256,256]{4,3,2,1,0:T(8,128)(2,1)S(1)}) custom-call(s32[4]{0:T(128)S(1)} %pad_add_fusion.1.refs_0_.src, bf16[1024,256]{1,0:T(8,128)(2,1)S(1)} %get-tuple-element.103.refs_1_.refs_0_, bf16[512,256]{1,0:T(8,128)(2,1)S(1)} %get-tuple-element.74.refs_2_, ...), custom_call_target="tpu_custom_call" | custom-call | tf_op jit(solution)/shard_map/conv_near/pallas_call | solution.py:406
  35.5 1.7 %collective-permute-start.10 = (bf16[512,256]{1,0:T(8,128)(2,1)S(1)}, bf16[512,256]{1,0:T(8,128)(2,1)S(1)}, u32[]{:S(2)}, u32[]{:S(2)}) collective-permute-start(bf16[512,256]{1,0:T(8,128)(2,1)S(1)} %get-tuple-element.73.refs_3_), channel_id=1, source_target_pairs={{0,2},{1,3},{2,0},{3,1},{4,6},{5,7},{6,4},{7,5},{8,10},{9,11},{10,... | collective-permute-start | bytes 786440 | tf_op jit(solution)/shard_map/ppermute | solution.py:27
  37.2 3.5 %conv_far.1 = (bf16[1040,256]{1,0:T(8,128)(2,1)S(1)}, f32[2,8,256]{2,1,0:T(8,128)S(1)}) custom-call(bf16[1024,256]{1,0:T(8,128)(2,1)S(1)} %get-tuple-element.32.refs_0_.refs_2_, bf16[512,256]{1,0:T(8,128)(2,1)S(1)} %collective-permute-done.7.refs_1_, bf16[1024,256]{1,0:T(8,128)(2,1)S(1)} %collective-permute-done.8.refs_2_.refs_3_, ...), custom_call_target="tpu_custom_call" | custom-call | tf_op jit(solution)/shard_map/conv_far/pallas_call | solution.py:426
  40.7 1.7 %collective-permute-start.12 = (f32[2,8,256]{2,1,0:T(8,128)S(1)}, f32[2,8,256]{2,1,0:T(8,128)S(1)}, u32[]{:S(2)}, u32[]{:S(2)}) collective-permute-start(f32[2,8,256]{2,1,0:T(8,128)S(1)} %get-tuple-element.37), channel_id=1, source_target_pairs={{0,2},{1,3},{2,0},{3,1},{4,6},{5,7},{6,4},{7,5},{8,10},{9,11},{10,... | collective-permute-start | bytes 49160 | tf_op jit(solution)/shard_map/ppermute | solution.py:27
  42.4 2.1 %collective-permute-done.12 = f32[2,8,256]{2,1,0:T(8,128)S(1)} collective-permute-done((f32[2,8,256]{2,1,0:T(8,128)S(1)}, f32[2,8,256]{2,1,0:T(8,128)S(1)}, u32[]{:S(2)}, u32[]{:S(2)}) %collective-permute-start.12) | collective-permute-done | bytes 16416 | tf_op jit(solution)/shard_map/ppermute | solution.py:27
  44.5 2.4 %collective-permute-start.13 = (f32[2,2,8,256]{3,2,1,0:T(8,128)S(1)}, f32[2,2,8,256]{3,2,1,0:T(8,128)S(1)}, u32[]{:S(2)}, u32[]{:S(2)}) collective-permute-start(f32[2,2,8,256]{3,2,1,0:T(8,128)S(1)} %pad_maximum_fusion), channel_id=1, source_target_pairs={{0,4},{4,0},{8,12},{12,8},{16,20},{20,16},{24,28},{28,24},{1,5},{5... | collective-permute-start | bytes 98312 | tf_op jit(solution)/shard_map/ppermute | solution.py:330
  46.9 1.7 %collective-permute-start.20 = (bf16[1040,256]{1,0:T(8,128)(2,1)S(1)}, bf16[1040,256]{1,0:T(8,128)(2,1)S(1)}, u32[]{:S(2)}, u32[]{:S(2)}) collective-permute-start(bf16[1040,256]{1,0:T(8,128)(2,1)S(1)} %get-tuple-element.38.refs_8_.refs_1_), channel_id=1, source_target_pairs={{0,2},{1,3},{2,0},{3,1},{4,6},{5,7},{6,4},{7,5},{8,10},{9,11},{10,... | collective-permute-start | bytes 1597448 | tf_op jit(solution)/shard_map/ppermute | solution.py:27
  48.9 5.8 %collective-permute-start.18 = (f32[2,2,8,256]{3,2,1,0:T(8,128)S(1)}, f32[2,2,8,256]{3,2,1,0:T(8,128)S(1)}, u32[]{:S(2)}, u32[]{:S(2)}) collective-permute-start(f32[2,2,8,256]{3,2,1,0:T(8,128)S(1)} %pad_maximum_fusion.4), channel_id=1, source_target_pairs={{0,24},{4,28},{8,16},{12,20},{16,8},{20,12},{24,0},{28,4},{1,25},{... | collective-permute-start | bytes 98312 | tf_op jit(solution)/shard_map/ppermute | solution.py:330
  55.3 1.4 %conv_edge.1.refs_2_ = bf16[512,256]{1,0:T(8,128)(2,1)S(1)} custom-call(bf16[1024,256]{1,0:T(8,128)(2,1)S(1)} %get-tuple-element.32.refs_0_.refs_2_, bf16[512,256]{1,0:T(8,128)(2,1)S(1)} %collective-permute-done.7.refs_1_, bf16[512,256]{1,0:T(8,128)(2,1)S(1)} %collective-permute-done.10.refs_2_, ...), custom_call_target="tpu_custom_call" | custom-call | tf_op jit(solution)/shard_map/conv_edge/pallas_call | solution.py:441
  56.8 1.6 %collective-permute-start.21 = (bf16[512,256]{1,0:T(8,128)(2,1)S(1)}, bf16[512,256]{1,0:T(8,128)(2,1)}, u32[]{:S(2)}, u32[]{:S(2)}) collective-permute-start(bf16[512,256]{1,0:T(8,128)(2,1)S(1)} %conv_edge.1.refs_2_), channel_id=1, source_target_pairs={{0,2},{1,3},{2,0},{3,1},{4,6},{5,7},{6,4},{7,5},{8,10},{9,11},{10,... | collective-permute-start | bytes 786440 | tf_op jit(solution)/shard_map/ppermute | solution.py:27
  59.6 2.4 %collective-permute-done.20.refs_1_ = bf16[1040,256]{1,0:T(8,128)(2,1)S(1)} collective-permute-done((bf16[1040,256]{1,0:T(8,128)(2,1)S(1)}, bf16[1040,256]{1,0:T(8,128)(2,1)S(1)}, u32[]{:S(2)}, u32[]{:S(2)}) %collective-permute-start.20) | collective-permute-done | bytes 532512 | tf_op jit(solution)/shard_map/ppermute | solution.py:27
  63.3 3.9 %collective-permute-done.21.refs_2_ = bf16[512,256]{1,0:T(8,128)(2,1)} collective-permute-done((bf16[512,256]{1,0:T(8,128)(2,1)S(1)}, bf16[512,256]{1,0:T(8,128)(2,1)}, u32[]{:S(2)}, u32[]{:S(2)}) %collective-permute-start.21) | collective-permute-done | bytes 262176 | tf_op jit(solution)/shard_map/ppermute | solution.py:27
  67.3 2.9 %fetch_two.1.refs_7_ = bf16[4,3,3,256,256]{4,3,2,1,0:T(8,128)(2,1)S(1)} custom-call(s32[4]{0:T(128)S(1)} %pad_add_fusion.1.refs_0_.src, bf16[3,3,1024,256]{3,2,1,0:T(8,128)(2,1)} %w.2), custom_call_target="tpu_custom_call" | custom-call | tf_op jit(solution)/shard_map/fetch_two/pallas_call | solution.py:456
  70.3 3.9 %two_near.1.refs_8_ = f32[3,4,256,256]{3,2,1,0:T(8,128)S(1)} custom-call(s32[2]{0:T(128)S(1)} %add_convert_fusion.1.refs_0_, bf16[1040,256]{1,0:T(8,128)(2,1)S(1)} %get-tuple-element.38.refs_8_.refs_1_, bf16[512,256]{1,0:T(8,128)(2,1)S(1)} %conv_edge.1.refs_2_, bf16[1040,256]{1,0:T(8,128)(2,1)} %collective-permute-done.14.refs_3_, ...), custom_call_target="tpu_custom_call" | custom-call | tf_op jit(solution)/shard_map/two_near/pallas_call | solution.py:465
  74.1 5.4 %two_far.1 = (f32[1024,256]{1,0:T(8,128)S(1)}, bf16[1040,256]{1,0:T(8,128)(2,1)}, f32[2,8,256]{2,1,0:T(8,128)S(1)}) custom-call(s32[2]{0:T(128)S(1)} %add_convert_fusion.1.refs_0_, bf16[1040,256]{1,0:T(8,128)(2,1)S(1)} %collective-permute-done.20.refs_1_, bf16[512,256]{1,0:T(8,128)(2,1)} %collective-permute-done.21.refs_2_, ...), custom_call_target="tpu_custom_call" | custom-call | tf_op jit(solution)/shard_map/two_far/pallas_call | solution.py:478
  80.6 1.7 %collective-permute-start.24 = (f32[2,8,256]{2,1,0:T(8,128)S(1)}, f32[2,8,256]{2,1,0:T(8,128)S(1)}, u32[]{:S(2)}, u32[]{:S(2)}) collective-permute-start(f32[2,8,256]{2,1,0:T(8,128)S(1)} %get-tuple-element.48), channel_id=1, source_target_pairs={{0,2},{1,3},{2,0},{3,1},{4,6},{5,7},{6,4},{7,5},{8,10},{9,11},{10,... | collective-permute-start | bytes 49160 | tf_op jit(solution)/shard_map/ppermute | solution.py:27
  82.3 2.0 %collective-permute-done.24 = f32[2,8,256]{2,1,0:T(8,128)S(1)} collective-permute-done((f32[2,8,256]{2,1,0:T(8,128)S(1)}, f32[2,8,256]{2,1,0:T(8,128)S(1)}, u32[]{:S(2)}, u32[]{:S(2)}) %collective-permute-start.24) | collective-permute-done | bytes 16416 | tf_op jit(solution)/shard_map/ppermute | solution.py:27
  84.4 1.7 %collective-permute-start.30 = (bf16[1040,256]{1,0:T(8,128)(2,1)}, bf16[1040,256]{1,0:T(8,128)(2,1)S(1)}, u32[]{:S(2)}, u32[]{:S(2)}) collective-permute-start(bf16[1040,256]{1,0:T(8,128)(2,1)} %get-tuple-element.49.refs_4_), channel_id=1, source_target_pairs={{0,2},{1,3},{2,0},{3,1},{4,6},{5,7},{6,4},{7,5},{8,10},{9,11},{10,... | collective-permute-start | bytes 1597448 | tf_op jit(solution)/shard_map/ppermute | solution.py:27
  86.1 2.1 %collective-permute-done.25 = f32[2,2,8,256]{3,2,1,0:T(8,128)S(1)} collective-permute-done((f32[2,2,8,256]{3,2,1,0:T(8,128)S(1)}, f32[2,2,8,256]{3,2,1,0:T(8,128)S(1)}, u32[]{:S(2)}, u32[]{:S(2)}) %collective-permute-start.25) | collective-permute-done | bytes 32800 | tf_op jit(solution)/shard_map/ppermute | solution.py:330
  88.2 3.9 %collective-permute-start.28 = (f32[2,2,8,256]{3,2,1,0:T(8,128)S(1)}, f32[2,2,8,256]{3,2,1,0:T(8,128)S(1)}, u32[]{:S(2)}, u32[]{:S(2)}) collective-permute-start(f32[2,2,8,256]{3,2,1,0:T(8,128)S(1)} %pad_maximum_fusion.5), channel_id=1, source_target_pairs={{0,24},{4,28},{8,16},{12,20},{16,8},{20,12},{24,0},{28,4},{1,25},{... | collective-permute-start | bytes 98312 | tf_op jit(solution)/shard_map/ppermute | solution.py:330
  93.0 2.8 %fetch_head.1.refs_12_ = bf16[4,256,2048]{2,1,0:T(8,128)(2,1)S(1)} custom-call(s32[4]{0:T(128)S(1)} %pad_add_fusion.1.refs_0_.src, bf16[1024,2048]{1,0:T(8,128)(2,1)} %w.3), custom_call_target="tpu_custom_call" | custom-call | tf_op jit(solution)/shard_map/fetch_head/pallas_call | solution.py:494
  98.5 1.5 %collective-permute-done.32 = f32[2,2,8,256]{3,2,1,0:T(8,128)S(1)} collective-permute-done((f32[2,2,8,256]{3,2,1,0:T(8,128)S(1)}, f32[2,2,8,256]{3,2,1,0:T(8,128)S(1)}, u32[]{:S(2)}, u32[]{:S(2)}) %collective-permute-start.32) | collective-permute-done | bytes 32800 | tf_op jit(solution)/shard_map/ppermute | solution.py:21
  99.9 9.8 %head.1 = f32[8,1024]{1,0:T(8,128)S(1)} custom-call(bf16[1024,256]{1,0:T(8,128)(2,1)S(1)} %get-tuple-element.103.refs_1_.refs_0_, bf16[1024,256]{1,0:T(8,128)(2,1)S(1)} %collective-permute-done.4.refs_4_.refs_1_, bf16[1024,256]{1,0:T(8,128)(2,1)S(1)} %get-tuple-element.32.refs_0_.refs_2_, bf16[1024,256]{1,0:T(8,128)(2,1)S(1)} %collective-permute-done.8.refs_2_.refs_3_, ...), custom_call_target="tpu_custom_call" | custom-call | tf_op jit(solution)/shard_map/head/pallas_call | solution.py:509
  111.1 1.8 %collective-permute-start.34 = (f32[3,1024]{1,0:T(4,128)S(1)}, f32[3,1024]{1,0:T(4,128)S(1)}, u32[]{:S(2)}, u32[]{:S(2)}) collective-permute-start(f32[3,1024]{1,0:T(4,128)S(1)} %pad_maximum_fusion.7), channel_id=1, source_target_pairs={{0,2},{1,3},{2,0},{3,1},{4,6},{5,7},{6,4},{7,5},{8,10},{9,11},{10,... | collective-permute-start | bytes 36872 | tf_op jit(solution)/shard_map/ppermute | solution.py:526
  112.9 2.0 %collective-permute-done.34 = f32[3,1024]{1,0:T(4,128)S(1)} collective-permute-done((f32[3,1024]{1,0:T(4,128)S(1)}, f32[3,1024]{1,0:T(4,128)S(1)}, u32[]{:S(2)}, u32[]{:S(2)}) %collective-permute-start.34) | collective-permute-done | bytes 12320 | tf_op jit(solution)/shard_map/ppermute | solution.py:526
  (125 shorter events, 14.5 us)
Async XLA Ops:
  7.8 9.1 %collective-permute-start.3 = (s32[512]{0:T(512)S(1)}, s32[512]{0:T(512)S(1)}, u32[]{:S(2)}, u32[]{:S(2)}) collective-permute-start(s32[512]{0:T(512)S(1)} %get-tuple-element.98), channel_id=1, source_target_pairs={{4,0},{8,4},{12,8},{16,12},{20,16},{24,20},{28,24},{5,1},{9,5},{13... | collective-permute-start | bytes 6152 | tf_op jit(solution)/shard_map/ppermute | solution.py:66
  9.1 15.9 %collective-permute-start = (bf16[1024,256]{1,0:T(8,128)(2,1)S(1)}, bf16[1024,256]{1,0:T(8,128)(2,1)S(1)}, u32[]{:S(2)}, u32[]{:S(2)}) collective-permute-start(bf16[1024,256]{1,0:T(8,128)(2,1)S(1)} %gather_fusion), channel_id=1, source_target_pairs={{0,2},{1,3},{2,0},{3,1},{4,6},{5,7},{6,4},{7,5},{8,10},{9,11},{10,... | collective-permute-start | bytes 1572872 | tf_op jit(solution)/shard_map/ppermute | solution.py:27
  12.2 12.7 %collective-permute-start.1 = (f32[5,8,256]{2,1,0:T(8,128)S(1)}, f32[5,8,256]{2,1,0:T(8,128)S(1)}, u32[]{:S(2)}, u32[]{:S(2)}) collective-permute-start(f32[5,8,256]{2,1,0:T(8,128)S(1)} %broadcast_in_dim.74), channel_id=1, source_target_pairs={{0,2},{1,3},{2,0},{3,1},{4,6},{5,7},{6,4},{7,5},{8,10},{9,11},{10,... | collective-permute-start | bytes 122888 | tf_op jit(solution)/shard_map/ppermute | solution.py:27
  12.3 5.8 %collective-permute-start.2 = (s32[512]{0:T(512)S(1)}, s32[512]{0:T(512)S(1)}, u32[]{:S(2)}, u32[]{:S(2)}) collective-permute-start(s32[512]{0:T(512)S(1)} %get-tuple-element.97), channel_id=1, source_target_pairs={{0,4},{4,8},{8,12},{12,16},{16,20},{20,24},{24,28},{1,5},{5,9},{9,... | collective-permute-start | bytes 6152 | tf_op jit(solution)/shard_map/ppermute | solution.py:61
  26.0 2.7 %collective-permute-start.4 = (bf16[1024,256]{1,0:T(8,128)(2,1)S(1)}, bf16[1024,256]{1,0:T(8,128)(2,1)S(1)}, u32[]{:S(2)}, u32[]{:S(2)}) collective-permute-start(bf16[1024,256]{1,0:T(8,128)(2,1)S(1)} %get-tuple-element.103.refs_1_.refs_0_), channel_id=1, source_target_pairs={{0,1},{1,0},{2,3},{3,2},{4,5},{5,4},{6,7},{7,6},{8,9},{9,8},{10,11... | collective-permute-start | bytes 1572872 | tf_op jit(solution)/shard_map/ppermute | solution.py:21
  26.1 2.5 %collective-permute-start.5 = (bf16[512,256]{1,0:T(8,128)(2,1)S(1)}, bf16[512,256]{1,0:T(8,128)(2,1)S(1)}, u32[]{:S(2)}, u32[]{:S(2)}) collective-permute-start(bf16[512,256]{1,0:T(8,128)(2,1)S(1)} %get-tuple-element.74.refs_2_), channel_id=1, source_target_pairs={{0,1},{1,0},{2,3},{3,2},{4,5},{5,4},{6,7},{7,6},{8,9},{9,8},{10,11... | collective-permute-start | bytes 786440 | tf_op jit(solution)/shard_map/ppermute | solution.py:21
  26.7 2.0 %collective-permute-start.6 = (bf16[512,256]{1,0:T(8,128)(2,1)S(1)}, bf16[512,256]{1,0:T(8,128)(2,1)S(1)}, u32[]{:S(2)}, u32[]{:S(2)}) collective-permute-start(bf16[512,256]{1,0:T(8,128)(2,1)S(1)} %get-tuple-element.73.refs_3_), channel_id=1, source_target_pairs={{0,1},{1,0},{2,3},{3,2},{4,5},{5,4},{6,7},{7,6},{8,9},{9,8},{10,11... | collective-permute-start | bytes 786440 | tf_op jit(solution)/shard_map/ppermute | solution.py:21
  26.8 8.6 %collective-permute-start.7 = (bf16[512,256]{1,0:T(8,128)(2,1)S(1)}, bf16[512,256]{1,0:T(8,128)(2,1)S(1)}, u32[]{:S(2)}, u32[]{:S(2)}) collective-permute-start(bf16[512,256]{1,0:T(8,128)(2,1)S(1)} %get-tuple-element.74.refs_2_), channel_id=1, source_target_pairs={{0,2},{1,3},{2,0},{3,1},{4,6},{5,7},{6,4},{7,5},{8,10},{9,11},{10,... | collective-permute-start | bytes 786440 | tf_op jit(solution)/shard_map/ppermute | solution.py:27
  34.8 2.4 %collective-permute-start.8 = (bf16[1024,256]{1,0:T(8,128)(2,1)S(1)}, bf16[1024,256]{1,0:T(8,128)(2,1)S(1)}, u32[]{:S(2)}, u32[]{:S(2)}) collective-permute-start(bf16[1024,256]{1,0:T(8,128)(2,1)S(1)} %get-tuple-element.32.refs_0_.refs_2_), channel_id=1, source_target_pairs={{0,1},{1,0},{2,3},{3,2},{4,5},{5,4},{6,7},{7,6},{8,9},{9,8},{10,11... | collective-permute-start | bytes 1572872 | tf_op jit(solution)/shard_map/ppermute | solution.py:21
  35.5 11.5 %collective-permute-start.10 = (bf16[512,256]{1,0:T(8,128)(2,1)S(1)}, bf16[512,256]{1,0:T(8,128)(2,1)S(1)}, u32[]{:S(2)}, u32[]{:S(2)}) collective-permute-start(bf16[512,256]{1,0:T(8,128)(2,1)S(1)} %get-tuple-element.73.refs_3_), channel_id=1, source_target_pairs={{0,2},{1,3},{2,0},{3,1},{4,6},{5,7},{6,4},{7,5},{8,10},{9,11},{10,... | collective-permute-start | bytes 786440 | tf_op jit(solution)/shard_map/ppermute | solution.py:27
  40.7 3.8 %collective-permute-start.12 = (f32[2,8,256]{2,1,0:T(8,128)S(1)}, f32[2,8,256]{2,1,0:T(8,128)S(1)}, u32[]{:S(2)}, u32[]{:S(2)}) collective-permute-start(f32[2,8,256]{2,1,0:T(8,128)S(1)} %get-tuple-element.37), channel_id=1, source_target_pairs={{0,2},{1,3},{2,0},{3,1},{4,6},{5,7},{6,4},{7,5},{8,10},{9,11},{10,... | collective-permute-start | bytes 49160 | tf_op jit(solution)/shard_map/ppermute | solution.py:27
  44.5 4.3 %collective-permute-start.13 = (f32[2,2,8,256]{3,2,1,0:T(8,128)S(1)}, f32[2,2,8,256]{3,2,1,0:T(8,128)S(1)}, u32[]{:S(2)}, u32[]{:S(2)}) collective-permute-start(f32[2,2,8,256]{3,2,1,0:T(8,128)S(1)} %pad_maximum_fusion), channel_id=1, source_target_pairs={{0,4},{4,0},{8,12},{12,8},{16,20},{20,16},{24,28},{28,24},{1,5},{5... | collective-permute-start | bytes 98312 | tf_op jit(solution)/shard_map/ppermute | solution.py:330
  46.9 8.4 %collective-permute-start.11 = (bf16[512,256]{1,0:T(8,128)(2,1)S(1)}, bf16[512,256]{1,0:T(8,128)(2,1)S(1)}, u32[]{:S(2)}, u32[]{:S(2)}) collective-permute-start(bf16[512,256]{1,0:T(8,128)(2,1)S(1)} %collective-permute-done.10.refs_2_), channel_id=1, source_target_pairs={{0,1},{1,0},{2,3},{3,2},{4,5},{5,4},{6,7},{7,6},{8,9},{9,8},{10,11... | collective-permute-start | bytes 786440 | tf_op jit(solution)/shard_map/ppermute | solution.py:21
  46.9 15.0 %collective-permute-start.20 = (bf16[1040,256]{1,0:T(8,128)(2,1)S(1)}, bf16[1040,256]{1,0:T(8,128)(2,1)S(1)}, u32[]{:S(2)}, u32[]{:S(2)}) collective-permute-start(bf16[1040,256]{1,0:T(8,128)(2,1)S(1)} %get-tuple-element.38.refs_8_.refs_1_), channel_id=1, source_target_pairs={{0,2},{1,3},{2,0},{3,1},{4,6},{5,7},{6,4},{7,5},{8,10},{9,11},{10,... | collective-permute-start | bytes 1597448 | tf_op jit(solution)/shard_map/ppermute | solution.py:27
  48.9 7.9 %collective-permute-start.18 = (f32[2,2,8,256]{3,2,1,0:T(8,128)S(1)}, f32[2,2,8,256]{3,2,1,0:T(8,128)S(1)}, u32[]{:S(2)}, u32[]{:S(2)}) collective-permute-start(f32[2,2,8,256]{3,2,1,0:T(8,128)S(1)} %pad_maximum_fusion.4), channel_id=1, source_target_pairs={{0,24},{4,28},{8,16},{12,20},{16,8},{20,12},{24,0},{28,4},{1,25},{... | collective-permute-start | bytes 98312 | tf_op jit(solution)/shard_map/ppermute | solution.py:330
  54.7 4.8 %collective-permute-start.17 = (f32[2,2,8,256]{3,2,1,0:T(8,128)S(1)}, f32[2,2,8,256]{3,2,1,0:T(8,128)S(1)}, u32[]{:S(2)}, u32[]{:S(2)}) collective-permute-start(f32[2,2,8,256]{3,2,1,0:T(8,128)S(1)} %pad_maximum_fusion.4), channel_id=1, source_target_pairs={{0,16},{4,20},{8,24},{12,28},{16,0},{20,4},{24,8},{28,12},{1,17},{... | collective-permute-start | bytes 98312 | tf_op jit(solution)/shard_map/ppermute | solution.py:330
  54.7 4.8 %collective-permute-start.16 = (f32[2,2,8,256]{3,2,1,0:T(8,128)S(1)}, f32[2,2,8,256]{3,2,1,0:T(8,128)S(1)}, u32[]{:S(2)}, u32[]{:S(2)}) collective-permute-start(f32[2,2,8,256]{3,2,1,0:T(8,128)S(1)} %pad_maximum_fusion.4), channel_id=1, source_target_pairs={{0,8},{4,12},{8,0},{12,4},{16,24},{20,28},{24,16},{28,20},{1,9},{5... | collective-permute-start | bytes 98312 | tf_op jit(solution)/shard_map/ppermute | solution.py:330
  55.3 14.9 %collective-permute-start.14 = (bf16[1040,256]{1,0:T(8,128)(2,1)S(1)}, bf16[1040,256]{1,0:T(8,128)(2,1)}, u32[]{:S(2)}, u32[]{:S(2)}) collective-permute-start(bf16[1040,256]{1,0:T(8,128)(2,1)S(1)} %get-tuple-element.38.refs_8_.refs_1_), channel_id=1, source_target_pairs={{0,1},{1,0},{2,3},{3,2},{4,5},{5,4},{6,7},{7,6},{8,9},{9,8},{10,11... | collective-permute-start | bytes 1597448 | tf_op jit(solution)/shard_map/ppermute | solution.py:21
  56.8 10.4 %collective-permute-start.21 = (bf16[512,256]{1,0:T(8,128)(2,1)S(1)}, bf16[512,256]{1,0:T(8,128)(2,1)}, u32[]{:S(2)}, u32[]{:S(2)}) collective-permute-start(bf16[512,256]{1,0:T(8,128)(2,1)S(1)} %conv_edge.1.refs_2_), channel_id=1, source_target_pairs={{0,2},{1,3},{2,0},{3,1},{4,6},{5,7},{6,4},{7,5},{8,10},{9,11},{10,... | collective-permute-start | bytes 786440 | tf_op jit(solution)/shard_map/ppermute | solution.py:27
  61.9 12.2 %collective-permute-start.22 = (bf16[1040,256]{1,0:T(8,128)(2,1)S(1)}, bf16[1040,256]{1,0:T(8,128)(2,1)}, u32[]{:S(2)}, u32[]{:S(2)}) collective-permute-start(bf16[1040,256]{1,0:T(8,128)(2,1)S(1)} %collective-permute-done.20.refs_1_), channel_id=1, source_target_pairs={{0,1},{1,0},{2,3},{3,2},{4,5},{5,4},{6,7},{7,6},{8,9},{9,8},{10,11... | collective-permute-start | bytes 1597448 | tf_op jit(solution)/shard_map/ppermute | solution.py:21
  61.9 8.3 %collective-permute-start.15 = (bf16[512,256]{1,0:T(8,128)(2,1)S(1)}, bf16[512,256]{1,0:T(8,128)(2,1)S(1)}, u32[]{:S(2)}, u32[]{:S(2)}) collective-permute-start(bf16[512,256]{1,0:T(8,128)(2,1)S(1)} %conv_edge.1.refs_2_), channel_id=1, source_target_pairs={{0,1},{1,0},{2,3},{3,2},{4,5},{5,4},{6,7},{7,6},{8,9},{9,8},{10,11... | collective-permute-start | bytes 786440 | tf_op jit(solution)/shard_map/ppermute | solution.py:21
  63.2 7.0 %collective-permute-start.19 = (f32[2,2,8,256]{3,2,1,0:T(8,128)S(1)}, f32[2,2,8,256]{3,2,1,0:T(8,128)S(1)}, u32[]{:S(2)}, u32[]{:S(2)}) collective-permute-start(f32[2,2,8,256]{3,2,1,0:T(8,128)S(1)} %pad_maximum_fusion.1), channel_id=1, source_target_pairs={{0,1},{1,0},{2,3},{3,2},{4,5},{5,4},{6,7},{7,6},{8,9},{9,8},{10,11... | collective-permute-start | bytes 98312 | tf_op jit(solution)/shard_map/ppermute | solution.py:21
  67.2 6.9 %collective-permute-start.23 = (bf16[512,256]{1,0:T(8,128)(2,1)}, bf16[512,256]{1,0:T(8,128)(2,1)S(1)}, u32[]{:S(2)}, u32[]{:S(2)}) collective-permute-start(bf16[512,256]{1,0:T(8,128)(2,1)} %collective-permute-done.21.refs_2_), channel_id=1, source_target_pairs={{0,1},{1,0},{2,3},{3,2},{4,5},{5,4},{6,7},{7,6},{8,9},{9,8},{10,11... | collective-permute-start | bytes 786440 | tf_op jit(solution)/shard_map/ppermute | solution.py:21
  80.6 3.7 %collective-permute-start.24 = (f32[2,8,256]{2,1,0:T(8,128)S(1)}, f32[2,8,256]{2,1,0:T(8,128)S(1)}, u32[]{:S(2)}, u32[]{:S(2)}) collective-permute-start(f32[2,8,256]{2,1,0:T(8,128)S(1)} %get-tuple-element.48), channel_id=1, source_target_pairs={{0,2},{1,3},{2,0},{3,1},{4,6},{5,7},{6,4},{7,5},{8,10},{9,11},{10,... | collective-permute-start | bytes 49160 | tf_op jit(solution)/shard_map/ppermute | solution.py:27
  84.3 3.9 %collective-permute-start.25 = (f32[2,2,8,256]{3,2,1,0:T(8,128)S(1)}, f32[2,2,8,256]{3,2,1,0:T(8,128)S(1)}, u32[]{:S(2)}, u32[]{:S(2)}) collective-permute-start(f32[2,2,8,256]{3,2,1,0:T(8,128)S(1)} %pad_maximum_fusion.2), channel_id=1, source_target_pairs={{0,4},{4,0},{8,12},{12,8},{16,20},{20,16},{24,28},{28,24},{1,5},{5... | collective-permute-start | bytes 98312 | tf_op jit(solution)/shard_map/ppermute | solution.py:330
  84.4 13.6 %collective-permute-start.30 = (bf16[1040,256]{1,0:T(8,128)(2,1)}, bf16[1040,256]{1,0:T(8,128)(2,1)S(1)}, u32[]{:S(2)}, u32[]{:S(2)}) collective-permute-start(bf16[1040,256]{1,0:T(8,128)(2,1)} %get-tuple-element.49.refs_4_), channel_id=1, source_target_pairs={{0,2},{1,3},{2,0},{3,1},{4,6},{5,7},{6,4},{7,5},{8,10},{9,11},{10,... | collective-permute-start | bytes 1597448 | tf_op jit(solution)/shard_map/ppermute | solution.py:27
  88.2 7.6 %collective-permute-start.28 = (f32[2,2,8,256]{3,2,1,0:T(8,128)S(1)}, f32[2,2,8,256]{3,2,1,0:T(8,128)S(1)}, u32[]{:S(2)}, u32[]{:S(2)}) collective-permute-start(f32[2,2,8,256]{3,2,1,0:T(8,128)S(1)} %pad_maximum_fusion.5), channel_id=1, source_target_pairs={{0,24},{4,28},{8,16},{12,20},{16,8},{20,12},{24,0},{28,4},{1,25},{... | collective-permute-start | bytes 98312 | tf_op jit(solution)/shard_map/ppermute | solution.py:330
  92.1 4.8 %collective-permute-start.27 = (f32[2,2,8,256]{3,2,1,0:T(8,128)S(1)}, f32[2,2,8,256]{3,2,1,0:T(8,128)S(1)}, u32[]{:S(2)}, u32[]{:S(2)}) collective-permute-start(f32[2,2,8,256]{3,2,1,0:T(8,128)S(1)} %pad_maximum_fusion.5), channel_id=1, source_target_pairs={{0,16},{4,20},{8,24},{12,28},{16,0},{20,4},{24,8},{28,12},{1,17},{... | collective-permute-start | bytes 98312 | tf_op jit(solution)/shard_map/ppermute | solution.py:330
  92.1 4.8 %collective-permute-start.26 = (f32[2,2,8,256]{3,2,1,0:T(8,128)S(1)}, f32[2,2,8,256]{3,2,1,0:T(8,128)S(1)}, u32[]{:S(2)}, u32[]{:S(2)}) collective-permute-start(f32[2,2,8,256]{3,2,1,0:T(8,128)S(1)} %pad_maximum_fusion.5), channel_id=1, source_target_pairs={{0,8},{4,12},{8,0},{12,4},{16,24},{20,28},{24,16},{28,20},{1,9},{5... | collective-permute-start | bytes 98312 | tf_op jit(solution)/shard_map/ppermute | solution.py:330
  93.0 7.0 %collective-permute-start.29 = (bf16[1040,256]{1,0:T(8,128)(2,1)}, bf16[1040,256]{1,0:T(8,128)(2,1)S(1)}, u32[]{:S(2)}, u32[]{:S(2)}) collective-permute-start(bf16[1040,256]{1,0:T(8,128)(2,1)} %get-tuple-element.49.refs_4_), channel_id=1, source_target_pairs={{0,1},{1,0},{2,3},{3,2},{4,5},{5,4},{6,7},{7,6},{8,9},{9,8},{10,11... | collective-permute-start | bytes 1597448 | tf_op jit(solution)/shard_map/ppermute | solution.py:21
  97.9 2.0 %collective-permute-start.31 = (bf16[1040,256]{1,0:T(8,128)(2,1)S(1)}, bf16[1040,256]{1,0:T(8,128)(2,1)S(1)}, u32[]{:S(2)}, u32[]{:S(2)}) collective-permute-start(bf16[1040,256]{1,0:T(8,128)(2,1)S(1)} %collective-permute-done.30.refs_6_), channel_id=1, source_target_pairs={{0,1},{1,0},{2,3},{3,2},{4,5},{5,4},{6,7},{7,6},{8,9},{9,8},{10,11... | collective-permute-start | bytes 1597448 | tf_op jit(solution)/shard_map/ppermute | solution.py:21
  111.1 3.8 %collective-permute-start.34 = (f32[3,1024]{1,0:T(4,128)S(1)}, f32[3,1024]{1,0:T(4,128)S(1)}, u32[]{:S(2)}, u32[]{:S(2)}) collective-permute-start(f32[3,1024]{1,0:T(4,128)S(1)} %pad_maximum_fusion.7), channel_id=1, source_target_pairs={{0,2},{1,3},{2,0},{3,1},{4,6},{5,7},{6,4},{7,5},{8,10},{9,11},{10,... | collective-permute-start | bytes 36872 | tf_op jit(solution)/shard_map/ppermute | solution.py:526
  (15 other events, 99.0 us)
where the time goes:
time: 116 us
  starting transfers between devices  38.3 us (33%)
  Pallas kernels  35.8 us (31%)
  waiting for transfers between devices  22 us (19%)
  local copies, waits for them, and re-layouts  14.4 us (12%)
  other arithmetic  4.1 us (4%)
    ppermute x9, starting transfers between devices, cross(): lax.ppermute(value, 'cols', [(i, (i + 2 * s) % n) for i in range(n)])  15 us
    ppermute x8, starting transfers between devices, over_rows(): others.append(lax.ppermute(stats, 'rows', move))  13.4 us
    ppermute x9, waiting for transfers between devices, cross(): lax.ppermute(value, 'cols', [(i, (i + 2 * s) % n) for i in range(n)])  12.4 us
    pallas_call x1, Pallas kernels, step_of(): pl.pallas_call(lambda *refs: head(count, n, tile, *refs), out_shape=jax.S...  9.82 us
    gather x1, local copies, waits for them, and re-layouts, look(): jnp.take(embed_table, jnp.maximum(codes - 2, 0), axis=0, mode='clip')  6.19 us
    gather x1, local copies, waits for them, and re-layouts, step_of(): looked = jnp.take(embed_table, token_ids.reshape(-1), axis=0, mode='clip')  6.18 us
    pallas_call x1, Pallas kernels, step_of(): pl.pallas_call(lambda *refs: conv_near(rows, width, *refs), out_shape=(ja...  6.09 us
    pallas_call x1, Pallas kernels, step_of(): pl.pallas_call(lambda *refs: second_far(rows, width, per_group, n - 2, *r...  5.4 us
  transfers between devices with their start and end apart: 35, of which 16 were waited for; matrix products, arithmetic and copies ran while one was open for 7% of the time, Pallas kernels for 18%

commit v1 on v0

--- a/solution.py
+++ b/solution.py
@@ -100,7 +100,7 @@
     return here + left + right
 
 
-def finish(parts, y_ref, packed_ref, stats_ref, rows, width, per_group):
+def finish(parts, y_ref, packed_ref, stats_ref, rows, width, per_group, out=None):
     here = y_ref.shape[1]
     count = rows * width
     total = jnp.zeros((1, here), F32)
@@ -108,6 +108,9 @@
         y = joined_taps(parts[0, i], parts[1, i], parts[2, i])
         y_ref[i * width : (i + 1) * width, :] = y
         total = total + tile_sum(y)
+    if out is not None:
+        copy = pltpu.make_async_copy(y_ref, *out)
+        copy.start()
     mean = total / count
     centre = mean.astype(BF16).astype(F32)
     square = jnp.zeros((1, here), F32)
@@ -134,6 +137,8 @@
     away = mean - mid[:1]
     stats_ref[0] = mid
     stats_ref[1] = over_group(spread + count * away * away)
+    if out is not None:
+        copy.wait()
 
 
 def reader(rows, width, main, inner, outer=None):
@@ -505,6 +510,7 @@
 
     ids = token_ids.reshape(-1, 1) - lax.axis_index("cols") * vocab_here
     ids = ids - lax.broadcasted_iota(jnp.int32, (1, 128), 1)
+    ids, features = lax.optimization_barrier((ids, features))
     tile = min(512, vocab_here)
     state = pl.pallas_call(
         lambda *refs: head(count, n, tile, *refs),

time: 116 us -> 121 us (1.043)
  waiting for transfers between devices: 22 us -> 34.3 us
  starting transfers between devices: 38.3 us -> 33.6 us
  Pallas kernels: 35.8 us -> 34.3 us
    ppermute x9, waiting for transfers between devices: 12.4 us -> 19.6 us  [cross(): lax.ppermute(value, 'cols', [(i, (i + 2 * s) % n) for i in range(n)])]
    ppermute x1, waiting for transfers between devices: 0.01 us -> 3.47 us  [downward(): return lax.ppermute(value, 'rows', [(i + 1, i) for i in range(n - 1)])]
    ppermute x8, starting transfers between devices: 13.4 us -> 10.9 us  [over_rows(): others.append(lax.ppermute(stats, 'rows', move))]
    ppermute x9, starting transfers between devices: 15 us -> 12.7 us  [cross(): lax.ppermute(value, 'cols', [(i, (i + 2 * s) % n) for i in range(n)])]
    ppermute x8, waiting for transfers between devices: 4.6 us -> 6.8 us  [over_rows(): others.append(lax.ppermute(stats, 'rows', move))]
    ppermute x1, waiting for transfers between devices: 1.27 us -> 0.01 us  [upward(): return lax.ppermute(value, 'rows', [(i, i + 1) for i in range(n - 1)])]
  transfers between devices with their start and end apart: 35 -> 35, of which waited for: 16 -> 16; matrix products, arithmetic and copies ran while one was open for 7% -> 7% of each run, Pallas kernels for 18% -> 17%
where the time goes in v1:
time: 121 us
  waiting for transfers between devices  34.3 us (28%)
  Pallas kernels  34.3 us (28%)
  starting transfers between devices  33.6 us (28%)
  local copies, waits for them, and re-layouts  13.3 us (11%)
  other arithmetic  4.11 us (3%)
    ppermute x9, waiting for transfers between devices, cross(): lax.ppermute(value, 'cols', [(i, (i + 2 * s) % n) for i in range(n)])  19.6 us
    ppermute x9, starting transfers between devices, cross(): lax.ppermute(value, 'cols', [(i, (i + 2 * s) % n) for i in range(n)])  12.7 us
    ppermute x8, starting transfers between devices, over_rows(): others.append(lax.ppermute(stats, 'rows', move))  10.9 us
    pallas_call x1, Pallas kernels, step_of(): pl.pallas_call(lambda *refs: head(count, n, tile, *refs), out_shape=jax.S...  8.66 us
    ppermute x8, waiting for transfers between devices, over_rows(): others.append(lax.ppermute(stats, 'rows', move))  6.8 us
    gather x1, local copies, waits for them, and re-layouts, look(): jnp.take(embed_table, jnp.maximum(codes - 2, 0), axis=0, mode='clip')  6.19 us
    gather x1, local copies, waits for them, and re-layouts, step_of(): looked = jnp.take(embed_table, token_ids.reshape(-1), axis=0, mode='clip')  6.18 us
    pallas_call x1, Pallas kernels, step_of(): pl.pallas_call(lambda *refs: conv_near(rows, width, *refs), out_shape=(ja...  6.08 us
  transfers between devices with their start and end apart: 35, of which 16 were waited for; matrix products, arithmetic and copies ran while one was open for 7% of the time, Pallas kernels for 17%

profile of v1, /device:TPU:0, one launch (start us, length us, event | category | flops | bytes accessed | tf_op | source)
XLA Modules:
  0.0 120.8 jit_solution(6242309679476233886)
XLA Ops:
  1.5 6.2 %gather_fusion = bf16[1024,256]{1,0:T(8,128)(2,1)S(1)} fusion(bf16[8192,256]{1,0:T(8,128)(2,1)} %param.15, s32[1024]{0:T(1024)S(1)} %broadcast_clamp_fusion.1), kind=kCustom, calls=%fused_computation | custom fusion | bytes 1052672 | tf_op jit(solution)/shard_map/jit(_take)/gather | solution.py:381
  7.8 4.9 %collective-permute-start.2 = (s32[512]{0:T(512)S(1)}, s32[512]{0:T(512)S(1)}, u32[]{:S(2)}, u32[]{:S(2)}) collective-permute-start(s32[512]{0:T(512)S(1)} %get-tuple-element.99), channel_id=1, source_target_pairs={{0,4},{4,8},{8,12},{12,16},{16,20},{20,24},{24,28},{1,5},{5,9},{9,... | collective-permute-start | bytes 6152 | tf_op jit(solution)/shard_map/ppermute | solution.py:61
  12.7 1.6 %collective-permute-start = (bf16[1024,256]{1,0:T(8,128)(2,1)S(1)}, bf16[1024,256]{1,0:T(8,128)(2,1)S(1)}, u32[]{:S(2)}, u32[]{:S(2)}) collective-permute-start(bf16[1024,256]{1,0:T(8,128)(2,1)S(1)} %gather_fusion), channel_id=1, source_target_pairs={{0,2},{1,3},{2,0},{3,1},{4,6},{5,7},{6,4},{7,5},{8,10},{9,11},{10,... | collective-permute-start | bytes 1572872 | tf_op jit(solution)/shard_map/ppermute | solution.py:27
  16.2 3.5 %collective-permute-done.3 = s32[512]{0:T(512)S(1)} collective-permute-done((s32[512]{0:T(512)S(1)}, s32[512]{0:T(512)S(1)}, u32[]{:S(2)}, u32[]{:S(2)}) %collective-permute-start.3) | collective-permute-done | bytes 2080 | tf_op jit(solution)/shard_map/ppermute | solution.py:66
  19.7 6.2 %gather_fusion.1 = bf16[1024,256]{1,0:T(8,128)(2,1)S(1)} fusion(bf16[8192,256]{1,0:T(8,128)(2,1)} %param.15, s32[1024]{0:T(1024)S(1)} %broadcast_clamp_fusion), kind=kCustom, calls=%fused_computation.1 | custom fusion | bytes 1052672 | tf_op jit(solution)/shard_map/jit(_take)/gather | solution.py:377
  28.9 1.5 %collective-permute-start.7 = (bf16[512,256]{1,0:T(8,128)(2,1)S(1)}, bf16[512,256]{1,0:T(8,128)(2,1)S(1)}, u32[]{:S(2)}, u32[]{:S(2)}) collective-permute-start(bf16[512,256]{1,0:T(8,128)(2,1)S(1)} %get-tuple-element.78.refs_2_), channel_id=1, source_target_pairs={{0,2},{1,3},{2,0},{3,1},{4,6},{5,7},{6,4},{7,5},{8,10},{9,11},{10,... | collective-permute-start | bytes 786440 | tf_op jit(solution)/shard_map/ppermute | solution.py:27
  30.8 6.1 %conv_near.1 = (f32[3,6,256,256]{3,2,1,0:T(8,128)S(1)}, bf16[2,3,3,256,256]{4,3,2,1,0:T(8,128)(2,1)S(1)}) custom-call(s32[4]{0:T(128)S(1)} %pad_add_fusion.1.refs_0_.src, bf16[1024,256]{1,0:T(8,128)(2,1)S(1)} %get-tuple-element.107.refs_1_.refs_0_, bf16[512,256]{1,0:T(8,128)(2,1)S(1)} %get-tuple-element.78.refs_2_, ...), custom_call_target="tpu_custom_call" | custom-call | tf_op jit(solution)/shard_map/conv_near/pallas_call | solution.py:411
  39.3 3.5 %conv_far.1 = (bf16[1040,256]{1,0:T(8,128)(2,1)S(1)}, f32[2,8,256]{2,1,0:T(8,128)S(1)}) custom-call(bf16[1024,256]{1,0:T(8,128)(2,1)S(1)} %get-tuple-element.34.refs_0_.refs_2_, bf16[512,256]{1,0:T(8,128)(2,1)S(1)} %collective-permute-done.7.refs_1_, bf16[1024,256]{1,0:T(8,128)(2,1)S(1)} %collective-permute-done.8.refs_2_.refs_3_, ...), custom_call_target="tpu_custom_call" | custom-call | tf_op jit(solution)/shard_map/conv_far/pallas_call | solution.py:431
  42.8 1.5 %collective-permute-start.12 = (f32[2,8,256]{2,1,0:T(8,128)S(1)}, f32[2,8,256]{2,1,0:T(8,128)S(1)}, u32[]{:S(2)}, u32[]{:S(2)}) collective-permute-start(f32[2,8,256]{2,1,0:T(8,128)S(1)} %get-tuple-element.39), channel_id=1, source_target_pairs={{0,2},{1,3},{2,0},{3,1},{4,6},{5,7},{6,4},{7,5},{8,10},{9,11},{10,... | collective-permute-start | bytes 49160 | tf_op jit(solution)/shard_map/ppermute | solution.py:27
  44.3 2.4 %collective-permute-done.12 = f32[2,8,256]{2,1,0:T(8,128)S(1)} collective-permute-done((f32[2,8,256]{2,1,0:T(8,128)S(1)}, f32[2,8,256]{2,1,0:T(8,128)S(1)}, u32[]{:S(2)}, u32[]{:S(2)}) %collective-permute-start.12) | collective-permute-done | bytes 16416 | tf_op jit(solution)/shard_map/ppermute | solution.py:27
  46.6 1.5 %collective-permute-start.13 = (f32[2,2,8,256]{3,2,1,0:T(8,128)S(1)}, f32[2,2,8,256]{3,2,1,0:T(8,128)S(1)}, u32[]{:S(2)}, u32[]{:S(2)}) collective-permute-start(f32[2,2,8,256]{3,2,1,0:T(8,128)S(1)} %pad_maximum_fusion), channel_id=1, source_target_pairs={{0,4},{4,0},{8,12},{12,8},{16,20},{20,16},{24,28},{28,24},{1,5},{5... | collective-permute-start | bytes 98312 | tf_op jit(solution)/shard_map/ppermute | solution.py:335
  48.2 1.5 %collective-permute-start.20 = (bf16[1040,256]{1,0:T(8,128)(2,1)S(1)}, bf16[1040,256]{1,0:T(8,128)(2,1)S(1)}, u32[]{:S(2)}, u32[]{:S(2)}) collective-permute-start(bf16[1040,256]{1,0:T(8,128)(2,1)S(1)} %get-tuple-element.40.refs_8_.refs_1_), channel_id=1, source_target_pairs={{0,2},{1,3},{2,0},{3,1},{4,6},{5,7},{6,4},{7,5},{8,10},{9,11},{10,... | collective-permute-start | bytes 1597448 | tf_op jit(solution)/shard_map/ppermute | solution.py:27
  50.6 1.6 %collective-permute-start.16 = (f32[2,2,8,256]{3,2,1,0:T(8,128)S(1)}, f32[2,2,8,256]{3,2,1,0:T(8,128)S(1)}, u32[]{:S(2)}, u32[]{:S(2)}) collective-permute-start(f32[2,2,8,256]{3,2,1,0:T(8,128)S(1)} %pad_maximum_fusion.4), channel_id=1, source_target_pairs={{0,8},{4,12},{8,0},{12,4},{16,24},{20,28},{24,16},{28,20},{1,9},{5... | collective-permute-start | bytes 98312 | tf_op jit(solution)/shard_map/ppermute | solution.py:335
  52.2 2.6 %collective-permute-start.17 = (f32[2,2,8,256]{3,2,1,0:T(8,128)S(1)}, f32[2,2,8,256]{3,2,1,0:T(8,128)S(1)}, u32[]{:S(2)}, u32[]{:S(2)}) collective-permute-start(f32[2,2,8,256]{3,2,1,0:T(8,128)S(1)} %pad_maximum_fusion.4), channel_id=1, source_target_pairs={{0,16},{4,20},{8,24},{12,28},{16,0},{20,4},{24,8},{28,12},{1,17},{... | collective-permute-start | bytes 98312 | tf_op jit(solution)/shard_map/ppermute | solution.py:335
  56.5 1.6 %collective-permute-start.21 = (bf16[512,256]{1,0:T(8,128)(2,1)S(1)}, bf16[512,256]{1,0:T(8,128)(2,1)}, u32[]{:S(2)}, u32[]{:S(2)}) collective-permute-start(bf16[512,256]{1,0:T(8,128)(2,1)S(1)} %conv_edge.1.refs_2_), channel_id=1, source_target_pairs={{0,2},{1,3},{2,0},{3,1},{4,6},{5,7},{6,4},{7,5},{8,10},{9,11},{10,... | collective-permute-start | bytes 786440 | tf_op jit(solution)/shard_map/ppermute | solution.py:27
  58.1 2.5 %collective-permute-done.18 = f32[2,2,8,256]{3,2,1,0:T(8,128)S(1)} collective-permute-done((f32[2,2,8,256]{3,2,1,0:T(8,128)S(1)}, f32[2,2,8,256]{3,2,1,0:T(8,128)S(1)}, u32[]{:S(2)}, u32[]{:S(2)}) %collective-permute-start.18) | collective-permute-done | bytes 32800 | tf_op jit(solution)/shard_map/ppermute | solution.py:335
  60.6 2.5 %collective-permute-done.20.refs_1_ = bf16[1040,256]{1,0:T(8,128)(2,1)S(1)} collective-permute-done((bf16[1040,256]{1,0:T(8,128)(2,1)S(1)}, bf16[1040,256]{1,0:T(8,128)(2,1)S(1)}, u32[]{:S(2)}, u32[]{:S(2)}) %collective-permute-start.20) | collective-permute-done | bytes 532512 | tf_op jit(solution)/shard_map/ppermute | solution.py:27
  64.5 3.9 %collective-permute-done.21.refs_2_ = bf16[512,256]{1,0:T(8,128)(2,1)} collective-permute-done((bf16[512,256]{1,0:T(8,128)(2,1)S(1)}, bf16[512,256]{1,0:T(8,128)(2,1)}, u32[]{:S(2)}, u32[]{:S(2)}) %collective-permute-start.21) | collective-permute-done | bytes 262176 | tf_op jit(solution)/shard_map/ppermute | solution.py:27
  68.5 2.9 %fetch_two.1.refs_7_ = bf16[4,3,3,256,256]{4,3,2,1,0:T(8,128)(2,1)S(1)} custom-call(s32[4]{0:T(128)S(1)} %pad_add_fusion.1.refs_0_.src, bf16[3,3,1024,256]{3,2,1,0:T(8,128)(2,1)} %w.2), custom_call_target="tpu_custom_call" | custom-call | tf_op jit(solution)/shard_map/fetch_two/pallas_call | solution.py:461
  71.5 3.8 %two_near.1.refs_8_ = f32[3,4,256,256]{3,2,1,0:T(8,128)S(1)} custom-call(s32[2]{0:T(128)S(1)} %add_convert_fusion.1.refs_0_, bf16[1040,256]{1,0:T(8,128)(2,1)S(1)} %get-tuple-element.40.refs_8_.refs_1_, bf16[512,256]{1,0:T(8,128)(2,1)S(1)} %conv_edge.1.refs_2_, bf16[1040,256]{1,0:T(8,128)(2,1)} %collective-permute-done.14.refs_3_, ...), custom_call_target="tpu_custom_call" | custom-call | tf_op jit(solution)/shard_map/two_near/pallas_call | solution.py:470
  75.3 5.0 %two_far.1 = (f32[1024,256]{1,0:T(8,128)S(1)}, bf16[1040,256]{1,0:T(8,128)(2,1)S(1)}, f32[2,8,256]{2,1,0:T(8,128)S(1)}) custom-call(s32[2]{0:T(128)S(1)} %add_convert_fusion.1.refs_0_, bf16[1040,256]{1,0:T(8,128)(2,1)S(1)} %collective-permute-done.20.refs_1_, bf16[512,256]{1,0:T(8,128)(2,1)} %collective-permute-done.21.refs_2_, ...), custom_call_target="tpu_custom_call" | custom-call | tf_op jit(solution)/shard_map/two_far/pallas_call | solution.py:483
  80.4 1.5 %collective-permute-start.24 = (f32[2,8,256]{2,1,0:T(8,128)S(1)}, f32[2,8,256]{2,1,0:T(8,128)S(1)}, u32[]{:S(2)}, u32[]{:S(2)}) collective-permute-start(f32[2,8,256]{2,1,0:T(8,128)S(1)} %get-tuple-element.50), channel_id=1, source_target_pairs={{0,2},{1,3},{2,0},{3,1},{4,6},{5,7},{6,4},{7,5},{8,10},{9,11},{10,... | collective-permute-start | bytes 49160 | tf_op jit(solution)/shard_map/ppermute | solution.py:27
  81.9 2.3 %collective-permute-done.24 = f32[2,8,256]{2,1,0:T(8,128)S(1)} collective-permute-done((f32[2,8,256]{2,1,0:T(8,128)S(1)}, f32[2,8,256]{2,1,0:T(8,128)S(1)}, u32[]{:S(2)}, u32[]{:S(2)}) %collective-permute-start.24) | collective-permute-done | bytes 16416 | tf_op jit(solution)/shard_map/ppermute | solution.py:27
  84.6 3.4 %collective-permute-done.25 = f32[2,2,8,256]{3,2,1,0:T(8,128)S(1)} collective-permute-done((f32[2,2,8,256]{3,2,1,0:T(8,128)S(1)}, f32[2,2,8,256]{3,2,1,0:T(8,128)S(1)}, u32[]{:S(2)}, u32[]{:S(2)}) %collective-permute-start.25) | collective-permute-done | bytes 32800 | tf_op jit(solution)/shard_map/ppermute | solution.py:335
  88.1 1.6 %collective-permute-start.26 = (f32[2,2,8,256]{3,2,1,0:T(8,128)S(1)}, f32[2,2,8,256]{3,2,1,0:T(8,128)S(1)}, u32[]{:S(2)}, u32[]{:S(2)}) collective-permute-start(f32[2,2,8,256]{3,2,1,0:T(8,128)S(1)} %pad_maximum_fusion.5), channel_id=1, source_target_pairs={{0,8},{4,12},{8,0},{12,4},{16,24},{20,28},{24,16},{28,20},{1,9},{5... | collective-permute-start | bytes 98312 | tf_op jit(solution)/shard_map/ppermute | solution.py:335
  90.9 1.7 %collective-permute-start.28 = (f32[2,2,8,256]{3,2,1,0:T(8,128)S(1)}, f32[2,2,8,256]{3,2,1,0:T(8,128)S(1)}, u32[]{:S(2)}, u32[]{:S(2)}) collective-permute-start(f32[2,2,8,256]{3,2,1,0:T(8,128)S(1)} %pad_maximum_fusion.5), channel_id=1, source_target_pairs={{0,24},{4,28},{8,16},{12,20},{16,8},{20,12},{24,0},{28,4},{1,25},{... | collective-permute-start | bytes 98312 | tf_op jit(solution)/shard_map/ppermute | solution.py:335
  92.7 1.6 %collective-permute-start.30 = (bf16[1040,256]{1,0:T(8,128)(2,1)S(1)}, bf16[1040,256]{1,0:T(8,128)(2,1)S(1)}, u32[]{:S(2)}, u32[]{:S(2)}) collective-permute-start(bf16[1040,256]{1,0:T(8,128)(2,1)S(1)} %get-tuple-element.52.refs_4_), channel_id=1, source_target_pairs={{0,2},{1,3},{2,0},{3,1},{4,6},{5,7},{6,4},{7,5},{8,10},{9,11},{10,... | collective-permute-start | bytes 1597448 | tf_op jit(solution)/shard_map/ppermute | solution.py:27
  94.3 2.8 %fetch_head.1.refs_12_ = bf16[4,256,2048]{2,1,0:T(8,128)(2,1)S(1)} custom-call(s32[4]{0:T(128)S(1)} %pad_add_fusion.1.refs_0_.src, bf16[1024,2048]{1,0:T(8,128)(2,1)} %w.3), custom_call_target="tpu_custom_call" | custom-call | tf_op jit(solution)/shard_map/fetch_head/pallas_call | solution.py:499
  97.1 7.0 %collective-permute-done.30.refs_6_ = bf16[1040,256]{1,0:T(8,128)(2,1)S(1)} collective-permute-done((bf16[1040,256]{1,0:T(8,128)(2,1)S(1)}, bf16[1040,256]{1,0:T(8,128)(2,1)S(1)}, u32[]{:S(2)}, u32[]{:S(2)}) %collective-permute-start.30) | collective-permute-done | bytes 532512 | tf_op jit(solution)/shard_map/ppermute | solution.py:27
  106.2 8.7 %head.1 = f32[8,1024]{1,0:T(8,128)S(1)} custom-call(bf16[1024,256]{1,0:T(8,128)(2,1)S(1)} %get-tuple-element.107.refs_1_.refs_0_, bf16[1024,256]{1,0:T(8,128)(2,1)S(1)} %collective-permute-done.4.refs_4_.refs_1_, bf16[1024,256]{1,0:T(8,128)(2,1)S(1)} %get-tuple-element.34.refs_0_.refs_2_, bf16[1024,256]{1,0:T(8,128)(2,1)S(1)} %collective-permute-done.8.refs_2_.refs_3_, ...), custom_call_target="tpu_custom_call" | custom-call | tf_op jit(solution)/shard_map/head/pallas_call | solution.py:515
  116.2 1.6 %collective-permute-start.34 = (f32[3,1024]{1,0:T(4,128)S(1)}, f32[3,1024]{1,0:T(4,128)S(1)}, u32[]{:S(2)}, u32[]{:S(2)}) collective-permute-start(f32[3,1024]{1,0:T(4,128)S(1)} %pad_maximum_fusion.7), channel_id=1, source_target_pairs={{0,2},{1,3},{2,0},{3,1},{4,6},{5,7},{6,4},{7,5},{8,10},{9,11},{10,... | collective-permute-start | bytes 36872 | tf_op jit(solution)/shard_map/ppermute | solution.py:532
  117.8 2.2 %collective-permute-done.34 = f32[3,1024]{1,0:T(4,128)S(1)} collective-permute-done((f32[3,1024]{1,0:T(4,128)S(1)}, f32[3,1024]{1,0:T(4,128)S(1)}, u32[]{:S(2)}, u32[]{:S(2)}) %collective-permute-start.34) | collective-permute-done | bytes 12320 | tf_op jit(solution)/shard_map/ppermute | solution.py:532
  (121 shorter events, 18.5 us)
Async XLA Ops:
  7.8 8.5 %collective-permute-start.2 = (s32[512]{0:T(512)S(1)}, s32[512]{0:T(512)S(1)}, u32[]{:S(2)}, u32[]{:S(2)}) collective-permute-start(s32[512]{0:T(512)S(1)} %get-tuple-element.99), channel_id=1, source_target_pairs={{0,4},{4,8},{8,12},{12,16},{16,20},{20,24},{24,28},{1,5},{5,9},{9,... | collective-permute-start | bytes 6152 | tf_op jit(solution)/shard_map/ppermute | solution.py:61
  12.7 14.3 %collective-permute-start = (bf16[1024,256]{1,0:T(8,128)(2,1)S(1)}, bf16[1024,256]{1,0:T(8,128)(2,1)S(1)}, u32[]{:S(2)}, u32[]{:S(2)}) collective-permute-start(bf16[1024,256]{1,0:T(8,128)(2,1)S(1)} %gather_fusion), channel_id=1, source_target_pairs={{0,2},{1,3},{2,0},{3,1},{4,6},{5,7},{6,4},{7,5},{8,10},{9,11},{10,... | collective-permute-start | bytes 1572872 | tf_op jit(solution)/shard_map/ppermute | solution.py:27
  14.2 5.5 %collective-permute-start.3 = (s32[512]{0:T(512)S(1)}, s32[512]{0:T(512)S(1)}, u32[]{:S(2)}, u32[]{:S(2)}) collective-permute-start(s32[512]{0:T(512)S(1)} %get-tuple-element.100), channel_id=1, source_target_pairs={{4,0},{8,4},{12,8},{16,12},{20,16},{24,20},{28,24},{5,1},{9,5},{13... | collective-permute-start | bytes 6152 | tf_op jit(solution)/shard_map/ppermute | solution.py:66
  15.6 11.4 %collective-permute-start.1 = (f32[5,8,256]{2,1,0:T(8,128)S(1)}, f32[5,8,256]{2,1,0:T(8,128)S(1)}, u32[]{:S(2)}, u32[]{:S(2)}) collective-permute-start(f32[5,8,256]{2,1,0:T(8,128)S(1)} %broadcast_in_dim.74), channel_id=1, source_target_pairs={{0,2},{1,3},{2,0},{3,1},{4,6},{5,7},{6,4},{7,5},{8,10},{9,11},{10,... | collective-permute-start | bytes 122888 | tf_op jit(solution)/shard_map/ppermute | solution.py:27
  28.1 2.7 %collective-permute-start.4 = (bf16[1024,256]{1,0:T(8,128)(2,1)S(1)}, bf16[1024,256]{1,0:T(8,128)(2,1)S(1)}, u32[]{:S(2)}, u32[]{:S(2)}) collective-permute-start(bf16[1024,256]{1,0:T(8,128)(2,1)S(1)} %get-tuple-element.107.refs_1_.refs_0_), channel_id=1, source_target_pairs={{0,1},{1,0},{2,3},{3,2},{4,5},{5,4},{6,7},{7,6},{8,9},{9,8},{10,11... | collective-permute-start | bytes 1572872 | tf_op jit(solution)/shard_map/ppermute | solution.py:21
  28.2 2.2 %collective-permute-start.5 = (bf16[512,256]{1,0:T(8,128)(2,1)S(1)}, bf16[512,256]{1,0:T(8,128)(2,1)S(1)}, u32[]{:S(2)}, u32[]{:S(2)}) collective-permute-start(bf16[512,256]{1,0:T(8,128)(2,1)S(1)} %get-tuple-element.78.refs_2_), channel_id=1, source_target_pairs={{0,1},{1,0},{2,3},{3,2},{4,5},{5,4},{6,7},{7,6},{8,9},{9,8},{10,11... | collective-permute-start | bytes 786440 | tf_op jit(solution)/shard_map/ppermute | solution.py:21
  28.8 2.0 %collective-permute-start.6 = (bf16[512,256]{1,0:T(8,128)(2,1)S(1)}, bf16[512,256]{1,0:T(8,128)(2,1)S(1)}, u32[]{:S(2)}, u32[]{:S(2)}) collective-permute-start(bf16[512,256]{1,0:T(8,128)(2,1)S(1)} %get-tuple-element.77.refs_3_), channel_id=1, source_target_pairs={{0,1},{1,0},{2,3},{3,2},{4,5},{5,4},{6,7},{7,6},{8,9},{9,8},{10,11... | collective-permute-start | bytes 786440 | tf_op jit(solution)/shard_map/ppermute | solution.py:21
  28.9 8.6 %collective-permute-start.7 = (bf16[512,256]{1,0:T(8,128)(2,1)S(1)}, bf16[512,256]{1,0:T(8,128)(2,1)S(1)}, u32[]{:S(2)}, u32[]{:S(2)}) collective-permute-start(bf16[512,256]{1,0:T(8,128)(2,1)S(1)} %get-tuple-element.78.refs_2_), channel_id=1, source_target_pairs={{0,2},{1,3},{2,0},{3,1},{4,6},{5,7},{6,4},{7,5},{8,10},{9,11},{10,... | collective-permute-start | bytes 786440 | tf_op jit(solution)/shard_map/ppermute | solution.py:27
  36.9 2.4 %collective-permute-start.8 = (bf16[1024,256]{1,0:T(8,128)(2,1)S(1)}, bf16[1024,256]{1,0:T(8,128)(2,1)S(1)}, u32[]{:S(2)}, u32[]{:S(2)}) collective-permute-start(bf16[1024,256]{1,0:T(8,128)(2,1)S(1)} %get-tuple-element.34.refs_0_.refs_2_), channel_id=1, source_target_pairs={{0,1},{1,0},{2,3},{3,2},{4,5},{5,4},{6,7},{7,6},{8,9},{9,8},{10,11... | collective-permute-start | bytes 1572872 | tf_op jit(solution)/shard_map/ppermute | solution.py:21
  37.6 10.6 %collective-permute-start.10 = (bf16[512,256]{1,0:T(8,128)(2,1)S(1)}, bf16[512,256]{1,0:T(8,128)(2,1)S(1)}, u32[]{:S(2)}, u32[]{:S(2)}) collective-permute-start(bf16[512,256]{1,0:T(8,128)(2,1)S(1)} %get-tuple-element.77.refs_3_), channel_id=1, source_target_pairs={{0,2},{1,3},{2,0},{3,1},{4,6},{5,7},{6,4},{7,5},{8,10},{9,11},{10,... | collective-permute-start | bytes 786440 | tf_op jit(solution)/shard_map/ppermute | solution.py:27
  42.8 3.9 %collective-permute-start.12 = (f32[2,8,256]{2,1,0:T(8,128)S(1)}, f32[2,8,256]{2,1,0:T(8,128)S(1)}, u32[]{:S(2)}, u32[]{:S(2)}) collective-permute-start(f32[2,8,256]{2,1,0:T(8,128)S(1)} %get-tuple-element.39), channel_id=1, source_target_pairs={{0,2},{1,3},{2,0},{3,1},{4,6},{5,7},{6,4},{7,5},{8,10},{9,11},{10,... | collective-permute-start | bytes 49160 | tf_op jit(solution)/shard_map/ppermute | solution.py:27
  46.6 3.9 %collective-permute-start.13 = (f32[2,2,8,256]{3,2,1,0:T(8,128)S(1)}, f32[2,2,8,256]{3,2,1,0:T(8,128)S(1)}, u32[]{:S(2)}, u32[]{:S(2)}) collective-permute-start(f32[2,2,8,256]{3,2,1,0:T(8,128)S(1)} %pad_maximum_fusion), channel_id=1, source_target_pairs={{0,4},{4,0},{8,12},{12,8},{16,20},{20,16},{24,28},{28,24},{1,5},{5... | collective-permute-start | bytes 98312 | tf_op jit(solution)/shard_map/ppermute | solution.py:335
  48.2 6.9 %collective-permute-start.11 = (bf16[512,256]{1,0:T(8,128)(2,1)S(1)}, bf16[512,256]{1,0:T(8,128)(2,1)S(1)}, u32[]{:S(2)}, u32[]{:S(2)}) collective-permute-start(bf16[512,256]{1,0:T(8,128)(2,1)S(1)} %collective-permute-done.10.refs_2_), channel_id=1, source_target_pairs={{0,1},{1,0},{2,3},{3,2},{4,5},{5,4},{6,7},{7,6},{8,9},{9,8},{10,11... | collective-permute-start | bytes 786440 | tf_op jit(solution)/shard_map/ppermute | solution.py:21
  48.2 15.0 %collective-permute-start.20 = (bf16[1040,256]{1,0:T(8,128)(2,1)S(1)}, bf16[1040,256]{1,0:T(8,128)(2,1)S(1)}, u32[]{:S(2)}, u32[]{:S(2)}) collective-permute-start(bf16[1040,256]{1,0:T(8,128)(2,1)S(1)} %get-tuple-element.40.refs_8_.refs_1_), channel_id=1, source_target_pairs={{0,2},{1,3},{2,0},{3,1},{4,6},{5,7},{6,4},{7,5},{8,10},{9,11},{10,... | collective-permute-start | bytes 1597448 | tf_op jit(solution)/shard_map/ppermute | solution.py:27
  50.6 5.9 %collective-permute-start.16 = (f32[2,2,8,256]{3,2,1,0:T(8,128)S(1)}, f32[2,2,8,256]{3,2,1,0:T(8,128)S(1)}, u32[]{:S(2)}, u32[]{:S(2)}) collective-permute-start(f32[2,2,8,256]{3,2,1,0:T(8,128)S(1)} %pad_maximum_fusion.4), channel_id=1, source_target_pairs={{0,8},{4,12},{8,0},{12,4},{16,24},{20,28},{24,16},{28,20},{1,9},{5... | collective-permute-start | bytes 98312 | tf_op jit(solution)/shard_map/ppermute | solution.py:335
  52.2 5.8 %collective-permute-start.17 = (f32[2,2,8,256]{3,2,1,0:T(8,128)S(1)}, f32[2,2,8,256]{3,2,1,0:T(8,128)S(1)}, u32[]{:S(2)}, u32[]{:S(2)}) collective-permute-start(f32[2,2,8,256]{3,2,1,0:T(8,128)S(1)} %pad_maximum_fusion.4), channel_id=1, source_target_pairs={{0,16},{4,20},{8,24},{12,28},{16,0},{20,4},{24,8},{28,12},{1,17},{... | collective-permute-start | bytes 98312 | tf_op jit(solution)/shard_map/ppermute | solution.py:335
  54.8 5.7 %collective-permute-start.18 = (f32[2,2,8,256]{3,2,1,0:T(8,128)S(1)}, f32[2,2,8,256]{3,2,1,0:T(8,128)S(1)}, u32[]{:S(2)}, u32[]{:S(2)}) collective-permute-start(f32[2,2,8,256]{3,2,1,0:T(8,128)S(1)} %pad_maximum_fusion.4), channel_id=1, source_target_pairs={{0,24},{4,28},{8,16},{12,20},{16,8},{20,12},{24,0},{28,4},{1,25},{... | collective-permute-start | bytes 98312 | tf_op jit(solution)/shard_map/ppermute | solution.py:335
  55.0 16.4 %collective-permute-start.14 = (bf16[1040,256]{1,0:T(8,128)(2,1)S(1)}, bf16[1040,256]{1,0:T(8,128)(2,1)}, u32[]{:S(2)}, u32[]{:S(2)}) collective-permute-start(bf16[1040,256]{1,0:T(8,128)(2,1)S(1)} %get-tuple-element.40.refs_8_.refs_1_), channel_id=1, source_target_pairs={{0,1},{1,0},{2,3},{3,2},{4,5},{5,4},{6,7},{7,6},{8,9},{9,8},{10,11... | collective-permute-start | bytes 1597448 | tf_op jit(solution)/shard_map/ppermute | solution.py:21
  56.5 11.9 %collective-permute-start.21 = (bf16[512,256]{1,0:T(8,128)(2,1)S(1)}, bf16[512,256]{1,0:T(8,128)(2,1)}, u32[]{:S(2)}, u32[]{:S(2)}) collective-permute-start(bf16[512,256]{1,0:T(8,128)(2,1)S(1)} %conv_edge.1.refs_2_), channel_id=1, source_target_pairs={{0,2},{1,3},{2,0},{3,1},{4,6},{5,7},{6,4},{7,5},{8,10},{9,11},{10,... | collective-permute-start | bytes 786440 | tf_op jit(solution)/shard_map/ppermute | solution.py:27
  63.1 12.2 %collective-permute-start.22 = (bf16[1040,256]{1,0:T(8,128)(2,1)S(1)}, bf16[1040,256]{1,0:T(8,128)(2,1)}, u32[]{:S(2)}, u32[]{:S(2)}) collective-permute-start(bf16[1040,256]{1,0:T(8,128)(2,1)S(1)} %collective-permute-done.20.refs_1_), channel_id=1, source_target_pairs={{0,1},{1,0},{2,3},{3,2},{4,5},{5,4},{6,7},{7,6},{8,9},{9,8},{10,11... | collective-permute-start | bytes 1597448 | tf_op jit(solution)/shard_map/ppermute | solution.py:21
  63.2 8.3 %collective-permute-start.15 = (bf16[512,256]{1,0:T(8,128)(2,1)S(1)}, bf16[512,256]{1,0:T(8,128)(2,1)S(1)}, u32[]{:S(2)}, u32[]{:S(2)}) collective-permute-start(bf16[512,256]{1,0:T(8,128)(2,1)S(1)} %conv_edge.1.refs_2_), channel_id=1, source_target_pairs={{0,1},{1,0},{2,3},{3,2},{4,5},{5,4},{6,7},{7,6},{8,9},{9,8},{10,11... | collective-permute-start | bytes 786440 | tf_op jit(solution)/shard_map/ppermute | solution.py:21
  64.4 7.0 %collective-permute-start.19 = (f32[2,2,8,256]{3,2,1,0:T(8,128)S(1)}, f32[2,2,8,256]{3,2,1,0:T(8,128)S(1)}, u32[]{:S(2)}, u32[]{:S(2)}) collective-permute-start(f32[2,2,8,256]{3,2,1,0:T(8,128)S(1)} %pad_maximum_fusion.1), channel_id=1, source_target_pairs={{0,1},{1,0},{2,3},{3,2},{4,5},{5,4},{6,7},{7,6},{8,9},{9,8},{10,11... | collective-permute-start | bytes 98312 | tf_op jit(solution)/shard_map/ppermute | solution.py:21
  68.4 6.9 %collective-permute-start.23 = (bf16[512,256]{1,0:T(8,128)(2,1)}, bf16[512,256]{1,0:T(8,128)(2,1)S(1)}, u32[]{:S(2)}, u32[]{:S(2)}) collective-permute-start(bf16[512,256]{1,0:T(8,128)(2,1)} %collective-permute-done.21.refs_2_), channel_id=1, source_target_pairs={{0,1},{1,0},{2,3},{3,2},{4,5},{5,4},{6,7},{7,6},{8,9},{9,8},{10,11... | collective-permute-start | bytes 786440 | tf_op jit(solution)/shard_map/ppermute | solution.py:21
  80.4 3.8 %collective-permute-start.24 = (f32[2,8,256]{2,1,0:T(8,128)S(1)}, f32[2,8,256]{2,1,0:T(8,128)S(1)}, u32[]{:S(2)}, u32[]{:S(2)}) collective-permute-start(f32[2,8,256]{2,1,0:T(8,128)S(1)} %get-tuple-element.50), channel_id=1, source_target_pairs={{0,2},{1,3},{2,0},{3,1},{4,6},{5,7},{6,4},{7,5},{8,10},{9,11},{10,... | collective-permute-start | bytes 49160 | tf_op jit(solution)/shard_map/ppermute | solution.py:27
  84.1 3.9 %collective-permute-start.25 = (f32[2,2,8,256]{3,2,1,0:T(8,128)S(1)}, f32[2,2,8,256]{3,2,1,0:T(8,128)S(1)}, u32[]{:S(2)}, u32[]{:S(2)}) collective-permute-start(f32[2,2,8,256]{3,2,1,0:T(8,128)S(1)} %pad_maximum_fusion.2), channel_id=1, source_target_pairs={{0,4},{4,0},{8,12},{12,8},{16,20},{20,16},{24,28},{28,24},{1,5},{5... | collective-permute-start | bytes 98312 | tf_op jit(solution)/shard_map/ppermute | solution.py:335
  88.1 9.0 %collective-permute-start.26 = (f32[2,2,8,256]{3,2,1,0:T(8,128)S(1)}, f32[2,2,8,256]{3,2,1,0:T(8,128)S(1)}, u32[]{:S(2)}, u32[]{:S(2)}) collective-permute-start(f32[2,2,8,256]{3,2,1,0:T(8,128)S(1)} %pad_maximum_fusion.5), channel_id=1, source_target_pairs={{0,8},{4,12},{8,0},{12,4},{16,24},{20,28},{24,16},{28,20},{1,9},{5... | collective-permute-start | bytes 98312 | tf_op jit(solution)/shard_map/ppermute | solution.py:335
  89.7 7.3 %collective-permute-start.27 = (f32[2,2,8,256]{3,2,1,0:T(8,128)S(1)}, f32[2,2,8,256]{3,2,1,0:T(8,128)S(1)}, u32[]{:S(2)}, u32[]{:S(2)}) collective-permute-start(f32[2,2,8,256]{3,2,1,0:T(8,128)S(1)} %pad_maximum_fusion.5), channel_id=1, source_target_pairs={{0,16},{4,20},{8,24},{12,28},{16,0},{20,4},{24,8},{28,12},{1,17},{... | collective-permute-start | bytes 98312 | tf_op jit(solution)/shard_map/ppermute | solution.py:335
  90.9 6.2 %collective-permute-start.28 = (f32[2,2,8,256]{3,2,1,0:T(8,128)S(1)}, f32[2,2,8,256]{3,2,1,0:T(8,128)S(1)}, u32[]{:S(2)}, u32[]{:S(2)}) collective-permute-start(f32[2,2,8,256]{3,2,1,0:T(8,128)S(1)} %pad_maximum_fusion.5), channel_id=1, source_target_pairs={{0,24},{4,28},{8,16},{12,20},{16,8},{20,12},{24,0},{28,4},{1,25},{... | collective-permute-start | bytes 98312 | tf_op jit(solution)/shard_map/ppermute | solution.py:335
  92.7 11.4 %collective-permute-start.30 = (bf16[1040,256]{1,0:T(8,128)(2,1)S(1)}, bf16[1040,256]{1,0:T(8,128)(2,1)S(1)}, u32[]{:S(2)}, u32[]{:S(2)}) collective-permute-start(bf16[1040,256]{1,0:T(8,128)(2,1)S(1)} %get-tuple-element.52.refs_4_), channel_id=1, source_target_pairs={{0,2},{1,3},{2,0},{3,1},{4,6},{5,7},{6,4},{7,5},{8,10},{9,11},{10,... | collective-permute-start | bytes 1597448 | tf_op jit(solution)/shard_map/ppermute | solution.py:27
  94.3 11.9 %collective-permute-start.29 = (bf16[1040,256]{1,0:T(8,128)(2,1)S(1)}, bf16[1040,256]{1,0:T(8,128)(2,1)S(1)}, u32[]{:S(2)}, u32[]{:S(2)}) collective-permute-start(bf16[1040,256]{1,0:T(8,128)(2,1)S(1)} %get-tuple-element.52.refs_4_), channel_id=1, source_target_pairs={{0,1},{1,0},{2,3},{3,2},{4,5},{5,4},{6,7},{7,6},{8,9},{9,8},{10,11... | collective-permute-start | bytes 1597448 | tf_op jit(solution)/shard_map/ppermute | solution.py:21
  104.2 2.0 %collective-permute-start.31 = (bf16[1040,256]{1,0:T(8,128)(2,1)S(1)}, bf16[1040,256]{1,0:T(8,128)(2,1)S(1)}, u32[]{:S(2)}, u32[]{:S(2)}) collective-permute-start(bf16[1040,256]{1,0:T(8,128)(2,1)S(1)} %collective-permute-done.30.refs_6_), channel_id=1, source_target_pairs={{0,1},{1,0},{2,3},{3,2},{4,5},{5,4},{6,7},{7,6},{8,9},{9,8},{10,11... | collective-permute-start | bytes 1597448 | tf_op jit(solution)/shard_map/ppermute | solution.py:21
  116.2 3.8 %collective-permute-start.34 = (f32[3,1024]{1,0:T(4,128)S(1)}, f32[3,1024]{1,0:T(4,128)S(1)}, u32[]{:S(2)}, u32[]{:S(2)}) collective-permute-start(f32[3,1024]{1,0:T(4,128)S(1)} %pad_maximum_fusion.7), channel_id=1, source_target_pairs={{0,2},{1,3},{2,0},{3,1},{4,6},{5,7},{6,4},{7,5},{8,10},{9,11},{10,... | collective-permute-start | bytes 36872 | tf_op jit(solution)/shard_map/ppermute | solution.py:532
  (13 other events, 105.5 us)

commit v2 on v1

--- a/solution.py
+++ b/solution.py
@@ -271,7 +271,7 @@
         for k in range(n):
             part = jnp.dot(
                 feat[k],
-                held[k, :, pl.ds(pl.multiple_of(t * tile, tile), tile)],
+                held[k, :, t * tile : (t + 1) * tile],
                 preferred_element_type=F32,
             )
             total = part if total is None else total + part
@@ -295,15 +295,9 @@
             summed[rows, :] = total
             picked[rows, :] = hit
 
-    multiply(0, 0)
-
-    def body(t, carry):
-        multiply(t, lax.rem(t, 2))
-        reduce(t - 1, lax.rem(t + 1, 2))
-        return carry
-
-    lax.fori_loop(1, tiles, body, 0)
-    reduce(tiles - 1, (tiles - 1) % 2)
+    for t in range(tiles):
+        multiply(t, t % 2)
+        reduce(t, t % 2)
     lane = lax.broadcasted_iota(jnp.int32, (128, 128), 1)
     for r in range(0, count, 128):
         rows = slice(r, r + 128)

time: 121 us -> 118 us (0.975)
  Pallas kernels: 34.3 us -> 31.2 us
    pallas_call x1, Pallas kernels: 8.66 us -> 5.59 us  [step_of(): pl.pallas_call(lambda *refs: head(count, n, tile, *refs), out_shape=jax.S...]
where the time goes in v2:
time: 118 us
  waiting for transfers between devices  34.3 us (29%)
  starting transfers between devices  33.6 us (28%)
  Pallas kernels  31.2 us (26%)
  local copies, waits for them, and re-layouts  13.3 us (11%)
  other arithmetic  4.11 us (3%)
    ppermute x9, waiting for transfers between devices, cross(): lax.ppermute(value, 'cols', [(i, (i + 2 * s) % n) for i in range(n)])  19.6 us
    ppermute x9, starting transfers between devices, cross(): lax.ppermute(value, 'cols', [(i, (i + 2 * s) % n) for i in range(n)])  12.7 us
    ppermute x8, starting transfers between devices, over_rows(): others.append(lax.ppermute(stats, 'rows', move))  10.9 us
    ppermute x8, waiting for transfers between devices, over_rows(): others.append(lax.ppermute(stats, 'rows', move))  6.8 us
    gather x1, local copies, waits for them, and re-layouts, look(): jnp.take(embed_table, jnp.maximum(codes - 2, 0), axis=0, mode='clip')  6.19 us
    gather x1, local copies, waits for them, and re-layouts, step_of(): looked = jnp.take(embed_table, token_ids.reshape(-1), axis=0, mode='clip')  6.18 us
    pallas_call x1, Pallas kernels, step_of(): pl.pallas_call(lambda *refs: conv_near(rows, width, *refs), out_shape=(ja...  6.08 us
    pallas_call x1, Pallas kernels, step_of(): pl.pallas_call(lambda *refs: head(count, n, tile, *refs), out_shape=jax.S...  5.59 us
  transfers between devices with their start and end apart: 35, of which 16 were waited for; matrix products, arithmetic and copies ran while one was open for 7% of the time, Pallas kernels for 17%

profile of v2, /device:TPU:0, one launch (start us, length us, event | category | flops | bytes accessed | tf_op | source)
XLA Modules:
  0.0 117.7 jit_solution(15110297592918253064)
XLA Ops:
  1.5 6.2 %gather_fusion = bf16[1024,256]{1,0:T(8,128)(2,1)S(1)} fusion(bf16[8192,256]{1,0:T(8,128)(2,1)} %param.15, s32[1024]{0:T(1024)S(1)} %broadcast_clamp_fusion.1), kind=kCustom, calls=%fused_computation | custom fusion | bytes 1052672 | tf_op jit(solution)/shard_map/jit(_take)/gather | solution.py:375
  7.8 4.9 %collective-permute-start.2 = (s32[512]{0:T(512)S(1)}, s32[512]{0:T(512)S(1)}, u32[]{:S(2)}, u32[]{:S(2)}) collective-permute-start(s32[512]{0:T(512)S(1)} %get-tuple-element.99), channel_id=1, source_target_pairs={{0,4},{4,8},{8,12},{12,16},{16,20},{20,24},{24,28},{1,5},{5,9},{9,... | collective-permute-start | bytes 6152 | tf_op jit(solution)/shard_map/ppermute | solution.py:61
  12.7 1.6 %collective-permute-start = (bf16[1024,256]{1,0:T(8,128)(2,1)S(1)}, bf16[1024,256]{1,0:T(8,128)(2,1)S(1)}, u32[]{:S(2)}, u32[]{:S(2)}) collective-permute-start(bf16[1024,256]{1,0:T(8,128)(2,1)S(1)} %gather_fusion), channel_id=1, source_target_pairs={{0,2},{1,3},{2,0},{3,1},{4,6},{5,7},{6,4},{7,5},{8,10},{9,11},{10,... | collective-permute-start | bytes 1572872 | tf_op jit(solution)/shard_map/ppermute | solution.py:27
  16.2 3.5 %collective-permute-done.3 = s32[512]{0:T(512)S(1)} collective-permute-done((s32[512]{0:T(512)S(1)}, s32[512]{0:T(512)S(1)}, u32[]{:S(2)}, u32[]{:S(2)}) %collective-permute-start.3) | collective-permute-done | bytes 2080 | tf_op jit(solution)/shard_map/ppermute | solution.py:66
  19.7 6.2 %gather_fusion.1 = bf16[1024,256]{1,0:T(8,128)(2,1)S(1)} fusion(bf16[8192,256]{1,0:T(8,128)(2,1)} %param.15, s32[1024]{0:T(1024)S(1)} %broadcast_clamp_fusion), kind=kCustom, calls=%fused_computation.1 | custom fusion | bytes 1052672 | tf_op jit(solution)/shard_map/jit(_take)/gather | solution.py:371
  28.9 1.5 %collective-permute-start.7 = (bf16[512,256]{1,0:T(8,128)(2,1)S(1)}, bf16[512,256]{1,0:T(8,128)(2,1)S(1)}, u32[]{:S(2)}, u32[]{:S(2)}) collective-permute-start(bf16[512,256]{1,0:T(8,128)(2,1)S(1)} %get-tuple-element.78.refs_2_), channel_id=1, source_target_pairs={{0,2},{1,3},{2,0},{3,1},{4,6},{5,7},{6,4},{7,5},{8,10},{9,11},{10,... | collective-permute-start | bytes 786440 | tf_op jit(solution)/shard_map/ppermute | solution.py:27
  30.8 6.1 %conv_near.1 = (f32[3,6,256,256]{3,2,1,0:T(8,128)S(1)}, bf16[2,3,3,256,256]{4,3,2,1,0:T(8,128)(2,1)S(1)}) custom-call(s32[4]{0:T(128)S(1)} %pad_add_fusion.1.refs_0_.src, bf16[1024,256]{1,0:T(8,128)(2,1)S(1)} %get-tuple-element.107.refs_1_.refs_0_, bf16[512,256]{1,0:T(8,128)(2,1)S(1)} %get-tuple-element.78.refs_2_, ...), custom_call_target="tpu_custom_call" | custom-call | tf_op jit(solution)/shard_map/conv_near/pallas_call | solution.py:405
  39.3 3.5 %conv_far.1 = (bf16[1040,256]{1,0:T(8,128)(2,1)S(1)}, f32[2,8,256]{2,1,0:T(8,128)S(1)}) custom-call(bf16[1024,256]{1,0:T(8,128)(2,1)S(1)} %get-tuple-element.34.refs_0_.refs_2_, bf16[512,256]{1,0:T(8,128)(2,1)S(1)} %collective-permute-done.7.refs_1_, bf16[1024,256]{1,0:T(8,128)(2,1)S(1)} %collective-permute-done.8.refs_2_.refs_3_, ...), custom_call_target="tpu_custom_call" | custom-call | tf_op jit(solution)/shard_map/conv_far/pallas_call | solution.py:425
  42.8 1.5 %collective-permute-start.12 = (f32[2,8,256]{2,1,0:T(8,128)S(1)}, f32[2,8,256]{2,1,0:T(8,128)S(1)}, u32[]{:S(2)}, u32[]{:S(2)}) collective-permute-start(f32[2,8,256]{2,1,0:T(8,128)S(1)} %get-tuple-element.39), channel_id=1, source_target_pairs={{0,2},{1,3},{2,0},{3,1},{4,6},{5,7},{6,4},{7,5},{8,10},{9,11},{10,... | collective-permute-start | bytes 49160 | tf_op jit(solution)/shard_map/ppermute | solution.py:27
  44.3 2.4 %collective-permute-done.12 = f32[2,8,256]{2,1,0:T(8,128)S(1)} collective-permute-done((f32[2,8,256]{2,1,0:T(8,128)S(1)}, f32[2,8,256]{2,1,0:T(8,128)S(1)}, u32[]{:S(2)}, u32[]{:S(2)}) %collective-permute-start.12) | collective-permute-done | bytes 16416 | tf_op jit(solution)/shard_map/ppermute | solution.py:27
  46.6 1.5 %collective-permute-start.13 = (f32[2,2,8,256]{3,2,1,0:T(8,128)S(1)}, f32[2,2,8,256]{3,2,1,0:T(8,128)S(1)}, u32[]{:S(2)}, u32[]{:S(2)}) collective-permute-start(f32[2,2,8,256]{3,2,1,0:T(8,128)S(1)} %pad_maximum_fusion), channel_id=1, source_target_pairs={{0,4},{4,0},{8,12},{12,8},{16,20},{20,16},{24,28},{28,24},{1,5},{5... | collective-permute-start | bytes 98312 | tf_op jit(solution)/shard_map/ppermute | solution.py:329
  48.2 1.5 %collective-permute-start.20 = (bf16[1040,256]{1,0:T(8,128)(2,1)S(1)}, bf16[1040,256]{1,0:T(8,128)(2,1)S(1)}, u32[]{:S(2)}, u32[]{:S(2)}) collective-permute-start(bf16[1040,256]{1,0:T(8,128)(2,1)S(1)} %get-tuple-element.40.refs_8_.refs_1_), channel_id=1, source_target_pairs={{0,2},{1,3},{2,0},{3,1},{4,6},{5,7},{6,4},{7,5},{8,10},{9,11},{10,... | collective-permute-start | bytes 1597448 | tf_op jit(solution)/shard_map/ppermute | solution.py:27
  50.6 1.6 %collective-permute-start.16 = (f32[2,2,8,256]{3,2,1,0:T(8,128)S(1)}, f32[2,2,8,256]{3,2,1,0:T(8,128)S(1)}, u32[]{:S(2)}, u32[]{:S(2)}) collective-permute-start(f32[2,2,8,256]{3,2,1,0:T(8,128)S(1)} %pad_maximum_fusion.4), channel_id=1, source_target_pairs={{0,8},{4,12},{8,0},{12,4},{16,24},{20,28},{24,16},{28,20},{1,9},{5... | collective-permute-start | bytes 98312 | tf_op jit(solution)/shard_map/ppermute | solution.py:329
  52.2 2.6 %collective-permute-start.17 = (f32[2,2,8,256]{3,2,1,0:T(8,128)S(1)}, f32[2,2,8,256]{3,2,1,0:T(8,128)S(1)}, u32[]{:S(2)}, u32[]{:S(2)}) collective-permute-start(f32[2,2,8,256]{3,2,1,0:T(8,128)S(1)} %pad_maximum_fusion.4), channel_id=1, source_target_pairs={{0,16},{4,20},{8,24},{12,28},{16,0},{20,4},{24,8},{28,12},{1,17},{... | collective-permute-start | bytes 98312 | tf_op jit(solution)/shard_map/ppermute | solution.py:329
  56.5 1.6 %collective-permute-start.21 = (bf16[512,256]{1,0:T(8,128)(2,1)S(1)}, bf16[512,256]{1,0:T(8,128)(2,1)}, u32[]{:S(2)}, u32[]{:S(2)}) collective-permute-start(bf16[512,256]{1,0:T(8,128)(2,1)S(1)} %conv_edge.1.refs_2_), channel_id=1, source_target_pairs={{0,2},{1,3},{2,0},{3,1},{4,6},{5,7},{6,4},{7,5},{8,10},{9,11},{10,... | collective-permute-start | bytes 786440 | tf_op jit(solution)/shard_map/ppermute | solution.py:27
  58.1 2.5 %collective-permute-done.18 = f32[2,2,8,256]{3,2,1,0:T(8,128)S(1)} collective-permute-done((f32[2,2,8,256]{3,2,1,0:T(8,128)S(1)}, f32[2,2,8,256]{3,2,1,0:T(8,128)S(1)}, u32[]{:S(2)}, u32[]{:S(2)}) %collective-permute-start.18) | collective-permute-done | bytes 32800 | tf_op jit(solution)/shard_map/ppermute | solution.py:329
  60.6 2.5 %collective-permute-done.20.refs_1_ = bf16[1040,256]{1,0:T(8,128)(2,1)S(1)} collective-permute-done((bf16[1040,256]{1,0:T(8,128)(2,1)S(1)}, bf16[1040,256]{1,0:T(8,128)(2,1)S(1)}, u32[]{:S(2)}, u32[]{:S(2)}) %collective-permute-start.20) | collective-permute-done | bytes 532512 | tf_op jit(solution)/shard_map/ppermute | solution.py:27
  64.5 3.9 %collective-permute-done.21.refs_2_ = bf16[512,256]{1,0:T(8,128)(2,1)} collective-permute-done((bf16[512,256]{1,0:T(8,128)(2,1)S(1)}, bf16[512,256]{1,0:T(8,128)(2,1)}, u32[]{:S(2)}, u32[]{:S(2)}) %collective-permute-start.21) | collective-permute-done | bytes 262176 | tf_op jit(solution)/shard_map/ppermute | solution.py:27
  68.5 2.9 %fetch_two.1.refs_7_ = bf16[4,3,3,256,256]{4,3,2,1,0:T(8,128)(2,1)S(1)} custom-call(s32[4]{0:T(128)S(1)} %pad_add_fusion.1.refs_0_.src, bf16[3,3,1024,256]{3,2,1,0:T(8,128)(2,1)} %w.2), custom_call_target="tpu_custom_call" | custom-call | tf_op jit(solution)/shard_map/fetch_two/pallas_call | solution.py:455
  71.5 3.8 %two_near.1.refs_8_ = f32[3,4,256,256]{3,2,1,0:T(8,128)S(1)} custom-call(s32[2]{0:T(128)S(1)} %add_convert_fusion.1.refs_0_, bf16[1040,256]{1,0:T(8,128)(2,1)S(1)} %get-tuple-element.40.refs_8_.refs_1_, bf16[512,256]{1,0:T(8,128)(2,1)S(1)} %conv_edge.1.refs_2_, bf16[1040,256]{1,0:T(8,128)(2,1)} %collective-permute-done.14.refs_3_, ...), custom_call_target="tpu_custom_call" | custom-call | tf_op jit(solution)/shard_map/two_near/pallas_call | solution.py:464
  75.3 5.0 %two_far.1 = (f32[1024,256]{1,0:T(8,128)S(1)}, bf16[1040,256]{1,0:T(8,128)(2,1)S(1)}, f32[2,8,256]{2,1,0:T(8,128)S(1)}) custom-call(s32[2]{0:T(128)S(1)} %add_convert_fusion.1.refs_0_, bf16[1040,256]{1,0:T(8,128)(2,1)S(1)} %collective-permute-done.20.refs_1_, bf16[512,256]{1,0:T(8,128)(2,1)} %collective-permute-done.21.refs_2_, ...), custom_call_target="tpu_custom_call" | custom-call | tf_op jit(solution)/shard_map/two_far/pallas_call | solution.py:477
  80.4 1.5 %collective-permute-start.24 = (f32[2,8,256]{2,1,0:T(8,128)S(1)}, f32[2,8,256]{2,1,0:T(8,128)S(1)}, u32[]{:S(2)}, u32[]{:S(2)}) collective-permute-start(f32[2,8,256]{2,1,0:T(8,128)S(1)} %get-tuple-element.50), channel_id=1, source_target_pairs={{0,2},{1,3},{2,0},{3,1},{4,6},{5,7},{6,4},{7,5},{8,10},{9,11},{10,... | collective-permute-start | bytes 49160 | tf_op jit(solution)/shard_map/ppermute | solution.py:27
  81.9 2.3 %collective-permute-done.24 = f32[2,8,256]{2,1,0:T(8,128)S(1)} collective-permute-done((f32[2,8,256]{2,1,0:T(8,128)S(1)}, f32[2,8,256]{2,1,0:T(8,128)S(1)}, u32[]{:S(2)}, u32[]{:S(2)}) %collective-permute-start.24) | collective-permute-done | bytes 16416 | tf_op jit(solution)/shard_map/ppermute | solution.py:27
  84.6 3.4 %collective-permute-done.25 = f32[2,2,8,256]{3,2,1,0:T(8,128)S(1)} collective-permute-done((f32[2,2,8,256]{3,2,1,0:T(8,128)S(1)}, f32[2,2,8,256]{3,2,1,0:T(8,128)S(1)}, u32[]{:S(2)}, u32[]{:S(2)}) %collective-permute-start.25) | collective-permute-done | bytes 32800 | tf_op jit(solution)/shard_map/ppermute | solution.py:329
  88.1 1.6 %collective-permute-start.26 = (f32[2,2,8,256]{3,2,1,0:T(8,128)S(1)}, f32[2,2,8,256]{3,2,1,0:T(8,128)S(1)}, u32[]{:S(2)}, u32[]{:S(2)}) collective-permute-start(f32[2,2,8,256]{3,2,1,0:T(8,128)S(1)} %pad_maximum_fusion.5), channel_id=1, source_target_pairs={{0,8},{4,12},{8,0},{12,4},{16,24},{20,28},{24,16},{28,20},{1,9},{5... | collective-permute-start | bytes 98312 | tf_op jit(solution)/shard_map/ppermute | solution.py:329
  90.9 1.7 %collective-permute-start.28 = (f32[2,2,8,256]{3,2,1,0:T(8,128)S(1)}, f32[2,2,8,256]{3,2,1,0:T(8,128)S(1)}, u32[]{:S(2)}, u32[]{:S(2)}) collective-permute-start(f32[2,2,8,256]{3,2,1,0:T(8,128)S(1)} %pad_maximum_fusion.5), channel_id=1, source_target_pairs={{0,24},{4,28},{8,16},{12,20},{16,8},{20,12},{24,0},{28,4},{1,25},{... | collective-permute-start | bytes 98312 | tf_op jit(solution)/shard_map/ppermute | solution.py:329
  92.7 1.6 %collective-permute-start.30 = (bf16[1040,256]{1,0:T(8,128)(2,1)S(1)}, bf16[1040,256]{1,0:T(8,128)(2,1)S(1)}, u32[]{:S(2)}, u32[]{:S(2)}) collective-permute-start(bf16[1040,256]{1,0:T(8,128)(2,1)S(1)} %get-tuple-element.52.refs_4_), channel_id=1, source_target_pairs={{0,2},{1,3},{2,0},{3,1},{4,6},{5,7},{6,4},{7,5},{8,10},{9,11},{10,... | collective-permute-start | bytes 1597448 | tf_op jit(solution)/shard_map/ppermute | solution.py:27
  94.3 2.8 %fetch_head.1.refs_12_ = bf16[4,256,2048]{2,1,0:T(8,128)(2,1)S(1)} custom-call(s32[4]{0:T(128)S(1)} %pad_add_fusion.1.refs_0_.src, bf16[1024,2048]{1,0:T(8,128)(2,1)} %w.3), custom_call_target="tpu_custom_call" | custom-call | tf_op jit(solution)/shard_map/fetch_head/pallas_call | solution.py:493
  97.1 7.0 %collective-permute-done.30.refs_6_ = bf16[1040,256]{1,0:T(8,128)(2,1)S(1)} collective-permute-done((bf16[1040,256]{1,0:T(8,128)(2,1)S(1)}, bf16[1040,256]{1,0:T(8,128)(2,1)S(1)}, u32[]{:S(2)}, u32[]{:S(2)}) %collective-permute-start.30) | collective-permute-done | bytes 532512 | tf_op jit(solution)/shard_map/ppermute | solution.py:27
  106.2 5.6 %head.1 = f32[8,1024]{1,0:T(8,128)S(1)} custom-call(bf16[1024,256]{1,0:T(8,128)(2,1)S(1)} %get-tuple-element.107.refs_1_.refs_0_, bf16[1024,256]{1,0:T(8,128)(2,1)S(1)} %collective-permute-done.4.refs_4_.refs_1_, bf16[1024,256]{1,0:T(8,128)(2,1)S(1)} %get-tuple-element.34.refs_0_.refs_2_, bf16[1024,256]{1,0:T(8,128)(2,1)S(1)} %collective-permute-done.8.refs_2_.refs_3_, ...), custom_call_target="tpu_custom_call" | custom-call | tf_op jit(solution)/shard_map/head/pallas_call | solution.py:509
  113.1 1.6 %collective-permute-start.34 = (f32[3,1024]{1,0:T(4,128)S(1)}, f32[3,1024]{1,0:T(4,128)S(1)}, u32[]{:S(2)}, u32[]{:S(2)}) collective-permute-start(f32[3,1024]{1,0:T(4,128)S(1)} %pad_maximum_fusion.7), channel_id=1, source_target_pairs={{0,2},{1,3},{2,0},{3,1},{4,6},{5,7},{6,4},{7,5},{8,10},{9,11},{10,... | collective-permute-start | bytes 36872 | tf_op jit(solution)/shard_map/ppermute | solution.py:526
  114.7 2.2 %collective-permute-done.34 = f32[3,1024]{1,0:T(4,128)S(1)} collective-permute-done((f32[3,1024]{1,0:T(4,128)S(1)}, f32[3,1024]{1,0:T(4,128)S(1)}, u32[]{:S(2)}, u32[]{:S(2)}) %collective-permute-start.34) | collective-permute-done | bytes 12320 | tf_op jit(solution)/shard_map/ppermute | solution.py:526
  (121 shorter events, 18.5 us)
Async XLA Ops:
  7.8 8.5 %collective-permute-start.2 = (s32[512]{0:T(512)S(1)}, s32[512]{0:T(512)S(1)}, u32[]{:S(2)}, u32[]{:S(2)}) collective-permute-start(s32[512]{0:T(512)S(1)} %get-tuple-element.99), channel_id=1, source_target_pairs={{0,4},{4,8},{8,12},{12,16},{16,20},{20,24},{24,28},{1,5},{5,9},{9,... | collective-permute-start | bytes 6152 | tf_op jit(solution)/shard_map/ppermute | solution.py:61
  12.7 14.3 %collective-permute-start = (bf16[1024,256]{1,0:T(8,128)(2,1)S(1)}, bf16[1024,256]{1,0:T(8,128)(2,1)S(1)}, u32[]{:S(2)}, u32[]{:S(2)}) collective-permute-start(bf16[1024,256]{1,0:T(8,128)(2,1)S(1)} %gather_fusion), channel_id=1, source_target_pairs={{0,2},{1,3},{2,0},{3,1},{4,6},{5,7},{6,4},{7,5},{8,10},{9,11},{10,... | collective-permute-start | bytes 1572872 | tf_op jit(solution)/shard_map/ppermute | solution.py:27
  14.2 5.5 %collective-permute-start.3 = (s32[512]{0:T(512)S(1)}, s32[512]{0:T(512)S(1)}, u32[]{:S(2)}, u32[]{:S(2)}) collective-permute-start(s32[512]{0:T(512)S(1)} %get-tuple-element.100), channel_id=1, source_target_pairs={{4,0},{8,4},{12,8},{16,12},{20,16},{24,20},{28,24},{5,1},{9,5},{13... | collective-permute-start | bytes 6152 | tf_op jit(solution)/shard_map/ppermute | solution.py:66
  15.6 11.4 %collective-permute-start.1 = (f32[5,8,256]{2,1,0:T(8,128)S(1)}, f32[5,8,256]{2,1,0:T(8,128)S(1)}, u32[]{:S(2)}, u32[]{:S(2)}) collective-permute-start(f32[5,8,256]{2,1,0:T(8,128)S(1)} %broadcast_in_dim.74), channel_id=1, source_target_pairs={{0,2},{1,3},{2,0},{3,1},{4,6},{5,7},{6,4},{7,5},{8,10},{9,11},{10,... | collective-permute-start | bytes 122888 | tf_op jit(solution)/shard_map/ppermute | solution.py:27
  28.1 2.7 %collective-permute-start.4 = (bf16[1024,256]{1,0:T(8,128)(2,1)S(1)}, bf16[1024,256]{1,0:T(8,128)(2,1)S(1)}, u32[]{:S(2)}, u32[]{:S(2)}) collective-permute-start(bf16[1024,256]{1,0:T(8,128)(2,1)S(1)} %get-tuple-element.107.refs_1_.refs_0_), channel_id=1, source_target_pairs={{0,1},{1,0},{2,3},{3,2},{4,5},{5,4},{6,7},{7,6},{8,9},{9,8},{10,11... | collective-permute-start | bytes 1572872 | tf_op jit(solution)/shard_map/ppermute | solution.py:21
  28.2 2.2 %collective-permute-start.5 = (bf16[512,256]{1,0:T(8,128)(2,1)S(1)}, bf16[512,256]{1,0:T(8,128)(2,1)S(1)}, u32[]{:S(2)}, u32[]{:S(2)}) collective-permute-start(bf16[512,256]{1,0:T(8,128)(2,1)S(1)} %get-tuple-element.78.refs_2_), channel_id=1, source_target_pairs={{0,1},{1,0},{2,3},{3,2},{4,5},{5,4},{6,7},{7,6},{8,9},{9,8},{10,11... | collective-permute-start | bytes 786440 | tf_op jit(solution)/shard_map/ppermute | solution.py:21
  28.8 2.0 %collective-permute-start.6 = (bf16[512,256]{1,0:T(8,128)(2,1)S(1)}, bf16[512,256]{1,0:T(8,128)(2,1)S(1)}, u32[]{:S(2)}, u32[]{:S(2)}) collective-permute-start(bf16[512,256]{1,0:T(8,128)(2,1)S(1)} %get-tuple-element.77.refs_3_), channel_id=1, source_target_pairs={{0,1},{1,0},{2,3},{3,2},{4,5},{5,4},{6,7},{7,6},{8,9},{9,8},{10,11... | collective-permute-start | bytes 786440 | tf_op jit(solution)/shard_map/ppermute | solution.py:21
  28.9 8.6 %collective-permute-start.7 = (bf16[512,256]{1,0:T(8,128)(2,1)S(1)}, bf16[512,256]{1,0:T(8,128)(2,1)S(1)}, u32[]{:S(2)}, u32[]{:S(2)}) collective-permute-start(bf16[512,256]{1,0:T(8,128)(2,1)S(1)} %get-tuple-element.78.refs_2_), channel_id=1, source_target_pairs={{0,2},{1,3},{2,0},{3,1},{4,6},{5,7},{6,4},{7,5},{8,10},{9,11},{10,... | collective-permute-start | bytes 786440 | tf_op jit(solution)/shard_map/ppermute | solution.py:27
  36.9 2.4 %collective-permute-start.8 = (bf16[1024,256]{1,0:T(8,128)(2,1)S(1)}, bf16[1024,256]{1,0:T(8,128)(2,1)S(1)}, u32[]{:S(2)}, u32[]{:S(2)}) collective-permute-start(bf16[1024,256]{1,0:T(8,128)(2,1)S(1)} %get-tuple-element.34.refs_0_.refs_2_), channel_id=1, source_target_pairs={{0,1},{1,0},{2,3},{3,2},{4,5},{5,4},{6,7},{7,6},{8,9},{9,8},{10,11... | collective-permute-start | bytes 1572872 | tf_op jit(solution)/shard_map/ppermute | solution.py:21
  37.6 10.6 %collective-permute-start.10 = (bf16[512,256]{1,0:T(8,128)(2,1)S(1)}, bf16[512,256]{1,0:T(8,128)(2,1)S(1)}, u32[]{:S(2)}, u32[]{:S(2)}) collective-permute-start(bf16[512,256]{1,0:T(8,128)(2,1)S(1)} %get-tuple-element.77.refs_3_), channel_id=1, source_target_pairs={{0,2},{1,3},{2,0},{3,1},{4,6},{5,7},{6,4},{7,5},{8,10},{9,11},{10,... | collective-permute-start | bytes 786440 | tf_op jit(solution)/shard_map/ppermute | solution.py:27
  42.8 3.9 %collective-permute-start.12 = (f32[2,8,256]{2,1,0:T(8,128)S(1)}, f32[2,8,256]{2,1,0:T(8,128)S(1)}, u32[]{:S(2)}, u32[]{:S(2)}) collective-permute-start(f32[2,8,256]{2,1,0:T(8,128)S(1)} %get-tuple-element.39), channel_id=1, source_target_pairs={{0,2},{1,3},{2,0},{3,1},{4,6},{5,7},{6,4},{7,5},{8,10},{9,11},{10,... | collective-permute-start | bytes 49160 | tf_op jit(solution)/shard_map/ppermute | solution.py:27
  46.6 3.9 %collective-permute-start.13 = (f32[2,2,8,256]{3,2,1,0:T(8,128)S(1)}, f32[2,2,8,256]{3,2,1,0:T(8,128)S(1)}, u32[]{:S(2)}, u32[]{:S(2)}) collective-permute-start(f32[2,2,8,256]{3,2,1,0:T(8,128)S(1)} %pad_maximum_fusion), channel_id=1, source_target_pairs={{0,4},{4,0},{8,12},{12,8},{16,20},{20,16},{24,28},{28,24},{1,5},{5... | collective-permute-start | bytes 98312 | tf_op jit(solution)/shard_map/ppermute | solution.py:329
  48.2 6.9 %collective-permute-start.11 = (bf16[512,256]{1,0:T(8,128)(2,1)S(1)}, bf16[512,256]{1,0:T(8,128)(2,1)S(1)}, u32[]{:S(2)}, u32[]{:S(2)}) collective-permute-start(bf16[512,256]{1,0:T(8,128)(2,1)S(1)} %collective-permute-done.10.refs_2_), channel_id=1, source_target_pairs={{0,1},{1,0},{2,3},{3,2},{4,5},{5,4},{6,7},{7,6},{8,9},{9,8},{10,11... | collective-permute-start | bytes 786440 | tf_op jit(solution)/shard_map/ppermute | solution.py:21
  48.2 15.0 %collective-permute-start.20 = (bf16[1040,256]{1,0:T(8,128)(2,1)S(1)}, bf16[1040,256]{1,0:T(8,128)(2,1)S(1)}, u32[]{:S(2)}, u32[]{:S(2)}) collective-permute-start(bf16[1040,256]{1,0:T(8,128)(2,1)S(1)} %get-tuple-element.40.refs_8_.refs_1_), channel_id=1, source_target_pairs={{0,2},{1,3},{2,0},{3,1},{4,6},{5,7},{6,4},{7,5},{8,10},{9,11},{10,... | collective-permute-start | bytes 1597448 | tf_op jit(solution)/shard_map/ppermute | solution.py:27
  50.6 5.9 %collective-permute-start.16 = (f32[2,2,8,256]{3,2,1,0:T(8,128)S(1)}, f32[2,2,8,256]{3,2,1,0:T(8,128)S(1)}, u32[]{:S(2)}, u32[]{:S(2)}) collective-permute-start(f32[2,2,8,256]{3,2,1,0:T(8,128)S(1)} %pad_maximum_fusion.4), channel_id=1, source_target_pairs={{0,8},{4,12},{8,0},{12,4},{16,24},{20,28},{24,16},{28,20},{1,9},{5... | collective-permute-start | bytes 98312 | tf_op jit(solution)/shard_map/ppermute | solution.py:329
  52.2 5.8 %collective-permute-start.17 = (f32[2,2,8,256]{3,2,1,0:T(8,128)S(1)}, f32[2,2,8,256]{3,2,1,0:T(8,128)S(1)}, u32[]{:S(2)}, u32[]{:S(2)}) collective-permute-start(f32[2,2,8,256]{3,2,1,0:T(8,128)S(1)} %pad_maximum_fusion.4), channel_id=1, source_target_pairs={{0,16},{4,20},{8,24},{12,28},{16,0},{20,4},{24,8},{28,12},{1,17},{... | collective-permute-start | bytes 98312 | tf_op jit(solution)/shard_map/ppermute | solution.py:329
  54.8 5.7 %collective-permute-start.18 = (f32[2,2,8,256]{3,2,1,0:T(8,128)S(1)}, f32[2,2,8,256]{3,2,1,0:T(8,128)S(1)}, u32[]{:S(2)}, u32[]{:S(2)}) collective-permute-start(f32[2,2,8,256]{3,2,1,0:T(8,128)S(1)} %pad_maximum_fusion.4), channel_id=1, source_target_pairs={{0,24},{4,28},{8,16},{12,20},{16,8},{20,12},{24,0},{28,4},{1,25},{... | collective-permute-start | bytes 98312 | tf_op jit(solution)/shard_map/ppermute | solution.py:329
  55.0 16.4 %collective-permute-start.14 = (bf16[1040,256]{1,0:T(8,128)(2,1)S(1)}, bf16[1040,256]{1,0:T(8,128)(2,1)}, u32[]{:S(2)}, u32[]{:S(2)}) collective-permute-start(bf16[1040,256]{1,0:T(8,128)(2,1)S(1)} %get-tuple-element.40.refs_8_.refs_1_), channel_id=1, source_target_pairs={{0,1},{1,0},{2,3},{3,2},{4,5},{5,4},{6,7},{7,6},{8,9},{9,8},{10,11... | collective-permute-start | bytes 1597448 | tf_op jit(solution)/shard_map/ppermute | solution.py:21
  56.5 11.9 %collective-permute-start.21 = (bf16[512,256]{1,0:T(8,128)(2,1)S(1)}, bf16[512,256]{1,0:T(8,128)(2,1)}, u32[]{:S(2)}, u32[]{:S(2)}) collective-permute-start(bf16[512,256]{1,0:T(8,128)(2,1)S(1)} %conv_edge.1.refs_2_), channel_id=1, source_target_pairs={{0,2},{1,3},{2,0},{3,1},{4,6},{5,7},{6,4},{7,5},{8,10},{9,11},{10,... | collective-permute-start | bytes 786440 | tf_op jit(solution)/shard_map/ppermute | solution.py:27
  63.1 12.2 %collective-permute-start.22 = (bf16[1040,256]{1,0:T(8,128)(2,1)S(1)}, bf16[1040,256]{1,0:T(8,128)(2,1)}, u32[]{:S(2)}, u32[]{:S(2)}) collective-permute-start(bf16[1040,256]{1,0:T(8,128)(2,1)S(1)} %collective-permute-done.20.refs_1_), channel_id=1, source_target_pairs={{0,1},{1,0},{2,3},{3,2},{4,5},{5,4},{6,7},{7,6},{8,9},{9,8},{10,11... | collective-permute-start | bytes 1597448 | tf_op jit(solution)/shard_map/ppermute | solution.py:21
  63.2 8.3 %collective-permute-start.15 = (bf16[512,256]{1,0:T(8,128)(2,1)S(1)}, bf16[512,256]{1,0:T(8,128)(2,1)S(1)}, u32[]{:S(2)}, u32[]{:S(2)}) collective-permute-start(bf16[512,256]{1,0:T(8,128)(2,1)S(1)} %conv_edge.1.refs_2_), channel_id=1, source_target_pairs={{0,1},{1,0},{2,3},{3,2},{4,5},{5,4},{6,7},{7,6},{8,9},{9,8},{10,11... | collective-permute-start | bytes 786440 | tf_op jit(solution)/shard_map/ppermute | solution.py:21
  64.4 7.0 %collective-permute-start.19 = (f32[2,2,8,256]{3,2,1,0:T(8,128)S(1)}, f32[2,2,8,256]{3,2,1,0:T(8,128)S(1)}, u32[]{:S(2)}, u32[]{:S(2)}) collective-permute-start(f32[2,2,8,256]{3,2,1,0:T(8,128)S(1)} %pad_maximum_fusion.1), channel_id=1, source_target_pairs={{0,1},{1,0},{2,3},{3,2},{4,5},{5,4},{6,7},{7,6},{8,9},{9,8},{10,11... | collective-permute-start | bytes 98312 | tf_op jit(solution)/shard_map/ppermute | solution.py:21
  68.4 6.9 %collective-permute-start.23 = (bf16[512,256]{1,0:T(8,128)(2,1)}, bf16[512,256]{1,0:T(8,128)(2,1)S(1)}, u32[]{:S(2)}, u32[]{:S(2)}) collective-permute-start(bf16[512,256]{1,0:T(8,128)(2,1)} %collective-permute-done.21.refs_2_), channel_id=1, source_target_pairs={{0,1},{1,0},{2,3},{3,2},{4,5},{5,4},{6,7},{7,6},{8,9},{9,8},{10,11... | collective-permute-start | bytes 786440 | tf_op jit(solution)/shard_map/ppermute | solution.py:21
  80.4 3.8 %collective-permute-start.24 = (f32[2,8,256]{2,1,0:T(8,128)S(1)}, f32[2,8,256]{2,1,0:T(8,128)S(1)}, u32[]{:S(2)}, u32[]{:S(2)}) collective-permute-start(f32[2,8,256]{2,1,0:T(8,128)S(1)} %get-tuple-element.50), channel_id=1, source_target_pairs={{0,2},{1,3},{2,0},{3,1},{4,6},{5,7},{6,4},{7,5},{8,10},{9,11},{10,... | collective-permute-start | bytes 49160 | tf_op jit(solution)/shard_map/ppermute | solution.py:27
  84.1 3.9 %collective-permute-start.25 = (f32[2,2,8,256]{3,2,1,0:T(8,128)S(1)}, f32[2,2,8,256]{3,2,1,0:T(8,128)S(1)}, u32[]{:S(2)}, u32[]{:S(2)}) collective-permute-start(f32[2,2,8,256]{3,2,1,0:T(8,128)S(1)} %pad_maximum_fusion.2), channel_id=1, source_target_pairs={{0,4},{4,0},{8,12},{12,8},{16,20},{20,16},{24,28},{28,24},{1,5},{5... | collective-permute-start | bytes 98312 | tf_op jit(solution)/shard_map/ppermute | solution.py:329
  88.1 9.0 %collective-permute-start.26 = (f32[2,2,8,256]{3,2,1,0:T(8,128)S(1)}, f32[2,2,8,256]{3,2,1,0:T(8,128)S(1)}, u32[]{:S(2)}, u32[]{:S(2)}) collective-permute-start(f32[2,2,8,256]{3,2,1,0:T(8,128)S(1)} %pad_maximum_fusion.5), channel_id=1, source_target_pairs={{0,8},{4,12},{8,0},{12,4},{16,24},{20,28},{24,16},{28,20},{1,9},{5... | collective-permute-start | bytes 98312 | tf_op jit(solution)/shard_map/ppermute | solution.py:329
  89.7 7.3 %collective-permute-start.27 = (f32[2,2,8,256]{3,2,1,0:T(8,128)S(1)}, f32[2,2,8,256]{3,2,1,0:T(8,128)S(1)}, u32[]{:S(2)}, u32[]{:S(2)}) collective-permute-start(f32[2,2,8,256]{3,2,1,0:T(8,128)S(1)} %pad_maximum_fusion.5), channel_id=1, source_target_pairs={{0,16},{4,20},{8,24},{12,28},{16,0},{20,4},{24,8},{28,12},{1,17},{... | collective-permute-start | bytes 98312 | tf_op jit(solution)/shard_map/ppermute | solution.py:329
  90.9 6.2 %collective-permute-start.28 = (f32[2,2,8,256]{3,2,1,0:T(8,128)S(1)}, f32[2,2,8,256]{3,2,1,0:T(8,128)S(1)}, u32[]{:S(2)}, u32[]{:S(2)}) collective-permute-start(f32[2,2,8,256]{3,2,1,0:T(8,128)S(1)} %pad_maximum_fusion.5), channel_id=1, source_target_pairs={{0,24},{4,28},{8,16},{12,20},{16,8},{20,12},{24,0},{28,4},{1,25},{... | collective-permute-start | bytes 98312 | tf_op jit(solution)/shard_map/ppermute | solution.py:329
  92.7 11.4 %collective-permute-start.30 = (bf16[1040,256]{1,0:T(8,128)(2,1)S(1)}, bf16[1040,256]{1,0:T(8,128)(2,1)S(1)}, u32[]{:S(2)}, u32[]{:S(2)}) collective-permute-start(bf16[1040,256]{1,0:T(8,128)(2,1)S(1)} %get-tuple-element.52.refs_4_), channel_id=1, source_target_pairs={{0,2},{1,3},{2,0},{3,1},{4,6},{5,7},{6,4},{7,5},{8,10},{9,11},{10,... | collective-permute-start | bytes 1597448 | tf_op jit(solution)/shard_map/ppermute | solution.py:27
  94.3 11.9 %collective-permute-start.29 = (bf16[1040,256]{1,0:T(8,128)(2,1)S(1)}, bf16[1040,256]{1,0:T(8,128)(2,1)S(1)}, u32[]{:S(2)}, u32[]{:S(2)}) collective-permute-start(bf16[1040,256]{1,0:T(8,128)(2,1)S(1)} %get-tuple-element.52.refs_4_), channel_id=1, source_target_pairs={{0,1},{1,0},{2,3},{3,2},{4,5},{5,4},{6,7},{7,6},{8,9},{9,8},{10,11... | collective-permute-start | bytes 1597448 | tf_op jit(solution)/shard_map/ppermute | solution.py:21
  104.2 2.0 %collective-permute-start.31 = (bf16[1040,256]{1,0:T(8,128)(2,1)S(1)}, bf16[1040,256]{1,0:T(8,128)(2,1)S(1)}, u32[]{:S(2)}, u32[]{:S(2)}) collective-permute-start(bf16[1040,256]{1,0:T(8,128)(2,1)S(1)} %collective-permute-done.30.refs_6_), channel_id=1, source_target_pairs={{0,1},{1,0},{2,3},{3,2},{4,5},{5,4},{6,7},{7,6},{8,9},{9,8},{10,11... | collective-permute-start | bytes 1597448 | tf_op jit(solution)/shard_map/ppermute | solution.py:21
  113.1 3.8 %collective-permute-start.34 = (f32[3,1024]{1,0:T(4,128)S(1)}, f32[3,1024]{1,0:T(4,128)S(1)}, u32[]{:S(2)}, u32[]{:S(2)}) collective-permute-start(f32[3,1024]{1,0:T(4,128)S(1)} %pad_maximum_fusion.7), channel_id=1, source_target_pairs={{0,2},{1,3},{2,0},{3,1},{4,6},{5,7},{6,4},{7,5},{8,10},{9,11},{10,... | collective-permute-start | bytes 36872 | tf_op jit(solution)/shard_map/ppermute | solution.py:526
  (13 other events, 105.5 us)

commit v3 on v2

--- a/solution.py
+++ b/solution.py
@@ -521,13 +521,14 @@
         compiler_params=params(16),
         name="head",
     )(*mains, *blocks, *norms, head_in, ids)
-    step = 1
-    while step < n:
-        other = lax.ppermute(state, "cols", [(i, i ^ step) for i in range(n)])
-        high = jnp.maximum(state[0], other[0])
-        total = state[1] * jnp.exp(state[0] - high) + other[1] * jnp.exp(other[0] - high)
-        state = jnp.stack([high, total, state[2] + other[2]])
-        step *= 2
+    states = [state] + [
+        lax.ppermute(state, "cols", [(i, i ^ k) for i in range(n)]) for k in range(n - 1, 0, -1)
+    ]
+    high = states[0][0]
+    for other in states[1:]:
+        high = jnp.maximum(high, other[0])
+    total = sum(t[1] * jnp.exp(t[0] - high) for t in states)
+    state = (high, total, sum(t[2] for t in states))
     logp = (state[2] - state[0] - jnp.log(state[1])).reshape(rows, width)
     slice_width = width // n
     token_logp = lax.dynamic_slice_in_dim(

time: 118 us -> 117 us (level)
  waiting for transfers between devices: 34.3 us -> 29.5 us
  starting transfers between devices: 33.6 us -> 37.6 us
    ppermute x1, waiting for transfers between devices: 3.47 us -> 0.01 us  [downward(): return lax.ppermute(value, 'rows', [(i + 1, i) for i in range(n - 1)])]
    ppermute x9, waiting for transfers between devices: 19.6 us -> 16.8 us  [cross(): lax.ppermute(value, 'cols', [(i, (i + 2 * s) % n) for i in range(n)])]
    ppermute x9, starting transfers between devices: 12.7 us -> 15.1 us  [cross(): lax.ppermute(value, 'cols', [(i, (i + 2 * s) % n) for i in range(n)])]
    ppermute x8, starting transfers between devices: 10.9 us -> 12.8 us  [over_rows(): others.append(lax.ppermute(stats, 'rows', move))]
    ppermute x2 -> x3, waiting for transfers between devices: 3.28 us -> 3.3 us  [step_of(): lax.ppermute(state, 'cols', [(i, i ^ k) for i in range(n)])]
  transfers between devices with their start and end apart: 35 -> 36, of which waited for: 16 -> 16; matrix products, arithmetic and copies ran while one was open for 7% -> 7% of each run, Pallas kernels for 17% -> 18%
where the time goes in v3:
time: 117 us
  starting transfers between devices  37.6 us (32%)
  Pallas kernels  31.2 us (27%)
  waiting for transfers between devices  29.5 us (25%)
  local copies, waits for them, and re-layouts  13.4 us (11%)
  other arithmetic  4.11 us (4%)
  between operations  1.17 us (1%)
    ppermute x9, waiting for transfers between devices, cross(): lax.ppermute(value, 'cols', [(i, (i + 2 * s) % n) for i in range(n)])  16.8 us
    ppermute x9, starting transfers between devices, cross(): lax.ppermute(value, 'cols', [(i, (i + 2 * s) % n) for i in range(n)])  15.1 us
    ppermute x8, starting transfers between devices, over_rows(): others.append(lax.ppermute(stats, 'rows', move))  12.8 us
    ppermute x8, waiting for transfers between devices, over_rows(): others.append(lax.ppermute(stats, 'rows', move))  7.65 us
    gather x1, local copies, waits for them, and re-layouts, look(): jnp.take(embed_table, jnp.maximum(codes - 2, 0), axis=0, mode='clip')  6.19 us
    gather x1, local copies, waits for them, and re-layouts, step_of(): looked = jnp.take(embed_table, token_ids.reshape(-1), axis=0, mode='clip')  6.18 us
    pallas_call x1, Pallas kernels, step_of(): pl.pallas_call(lambda *refs: conv_near(rows, width, *refs), out_shape=(ja...  6.09 us
    pallas_call x1, Pallas kernels, step_of(): pl.pallas_call(lambda *refs: head(count, n, tile, *refs), out_shape=jax.S...  5.59 us
  transfers between devices with their start and end apart: 36, of which 16 were waited for; matrix products, arithmetic and copies ran while one was open for 7% of the time, Pallas kernels for 18%

profile of v3, /device:TPU:0, one launch (start us, length us, event | category | flops | bytes accessed | tf_op | source)
XLA Modules:
  0.0 116.9 jit_solution(12882381013288676620)
XLA Ops:
  1.5 6.2 %gather_fusion = bf16[1024,256]{1,0:T(8,128)(2,1)S(1)} fusion(bf16[8192,256]{1,0:T(8,128)(2,1)} %param.15, s32[1024]{0:T(1024)S(1)} %broadcast_clamp_fusion.1), kind=kCustom, calls=%fused_computation | custom fusion | bytes 1052672 | tf_op jit(solution)/shard_map/jit(_take)/gather | solution.py:375
  9.1 3.0 %collective-permute-start = (bf16[1024,256]{1,0:T(8,128)(2,1)S(1)}, bf16[1024,256]{1,0:T(8,128)(2,1)S(1)}, u32[]{:S(2)}, u32[]{:S(2)}) collective-permute-start(bf16[1024,256]{1,0:T(8,128)(2,1)S(1)} %gather_fusion), channel_id=1, source_target_pairs={{0,2},{1,3},{2,0},{3,1},{4,6},{5,7},{6,4},{7,5},{8,10},{9,11},{10,... | collective-permute-start | bytes 1572872 | tf_op jit(solution)/shard_map/ppermute | solution.py:27
  12.1 4.5 %collective-permute-start.2 = (s32[512]{0:T(512)S(1)}, s32[512]{0:T(512)S(1)}, u32[]{:S(2)}, u32[]{:S(2)}) collective-permute-start(s32[512]{0:T(512)S(1)} %get-tuple-element.93), channel_id=1, source_target_pairs={{0,4},{4,8},{8,12},{12,16},{16,20},{20,24},{24,28},{1,5},{5,9},{9,... | collective-permute-start | bytes 6152 | tf_op jit(solution)/shard_map/ppermute | solution.py:61
  18.0 6.2 %gather_fusion.1 = bf16[1024,256]{1,0:T(8,128)(2,1)S(1)} fusion(bf16[8192,256]{1,0:T(8,128)(2,1)} %param.15, s32[1024]{0:T(1024)S(1)} %broadcast_clamp_fusion), kind=kCustom, calls=%fused_computation.1 | custom fusion | bytes 1052672 | tf_op jit(solution)/shard_map/jit(_take)/gather | solution.py:371
  26.8 1.7 %collective-permute-start.7 = (bf16[512,256]{1,0:T(8,128)(2,1)S(1)}, bf16[512,256]{1,0:T(8,128)(2,1)S(1)}, u32[]{:S(2)}, u32[]{:S(2)}) collective-permute-start(bf16[512,256]{1,0:T(8,128)(2,1)S(1)} %get-tuple-element.78.refs_2_), channel_id=1, source_target_pairs={{0,2},{1,3},{2,0},{3,1},{4,6},{5,7},{6,4},{7,5},{8,10},{9,11},{10,... | collective-permute-start | bytes 786440 | tf_op jit(solution)/shard_map/ppermute | solution.py:27
  28.7 6.1 %conv_near.1 = (f32[3,6,256,256]{3,2,1,0:T(8,128)S(1)}, bf16[2,3,3,256,256]{4,3,2,1,0:T(8,128)(2,1)S(1)}) custom-call(s32[4]{0:T(128)S(1)} %pad_add_fusion.1.refs_0_.src, bf16[1024,256]{1,0:T(8,128)(2,1)S(1)} %get-tuple-element.101.refs_1_.refs_0_, bf16[512,256]{1,0:T(8,128)(2,1)S(1)} %get-tuple-element.78.refs_2_, ...), custom_call_target="tpu_custom_call" | custom-call | tf_op jit(solution)/shard_map/conv_near/pallas_call | solution.py:405
  35.5 1.7 %collective-permute-start.10 = (bf16[512,256]{1,0:T(8,128)(2,1)S(1)}, bf16[512,256]{1,0:T(8,128)(2,1)S(1)}, u32[]{:S(2)}, u32[]{:S(2)}) collective-permute-start(bf16[512,256]{1,0:T(8,128)(2,1)S(1)} %get-tuple-element.77.refs_3_), channel_id=1, source_target_pairs={{0,2},{1,3},{2,0},{3,1},{4,6},{5,7},{6,4},{7,5},{8,10},{9,11},{10,... | collective-permute-start | bytes 786440 | tf_op jit(solution)/shard_map/ppermute | solution.py:27
  37.2 3.5 %conv_far.1 = (bf16[1040,256]{1,0:T(8,128)(2,1)S(1)}, f32[2,8,256]{2,1,0:T(8,128)S(1)}) custom-call(bf16[1024,256]{1,0:T(8,128)(2,1)S(1)} %get-tuple-element.34.refs_0_.refs_2_, bf16[512,256]{1,0:T(8,128)(2,1)S(1)} %collective-permute-done.7.refs_1_, bf16[1024,256]{1,0:T(8,128)(2,1)S(1)} %collective-permute-done.8.refs_2_.refs_3_, ...), custom_call_target="tpu_custom_call" | custom-call | tf_op jit(solution)/shard_map/conv_far/pallas_call | solution.py:425
  40.7 1.7 %collective-permute-start.12 = (f32[2,8,256]{2,1,0:T(8,128)S(1)}, f32[2,8,256]{2,1,0:T(8,128)S(1)}, u32[]{:S(2)}, u32[]{:S(2)}) collective-permute-start(f32[2,8,256]{2,1,0:T(8,128)S(1)} %get-tuple-element.39), channel_id=1, source_target_pairs={{0,2},{1,3},{2,0},{3,1},{4,6},{5,7},{6,4},{7,5},{8,10},{9,11},{10,... | collective-permute-start | bytes 49160 | tf_op jit(solution)/shard_map/ppermute | solution.py:27
  42.4 2.1 %collective-permute-done.12 = f32[2,8,256]{2,1,0:T(8,128)S(1)} collective-permute-done((f32[2,8,256]{2,1,0:T(8,128)S(1)}, f32[2,8,256]{2,1,0:T(8,128)S(1)}, u32[]{:S(2)}, u32[]{:S(2)}) %collective-permute-start.12) | collective-permute-done | bytes 16416 | tf_op jit(solution)/shard_map/ppermute | solution.py:27
  44.5 2.4 %collective-permute-start.13 = (f32[2,2,8,256]{3,2,1,0:T(8,128)S(1)}, f32[2,2,8,256]{3,2,1,0:T(8,128)S(1)}, u32[]{:S(2)}, u32[]{:S(2)}) collective-permute-start(f32[2,2,8,256]{3,2,1,0:T(8,128)S(1)} %pad_maximum_fusion), channel_id=1, source_target_pairs={{0,4},{4,0},{8,12},{12,8},{16,20},{20,16},{24,28},{28,24},{1,5},{5... | collective-permute-start | bytes 98312 | tf_op jit(solution)/shard_map/ppermute | solution.py:329
  46.9 1.7 %collective-permute-start.20 = (bf16[1040,256]{1,0:T(8,128)(2,1)S(1)}, bf16[1040,256]{1,0:T(8,128)(2,1)S(1)}, u32[]{:S(2)}, u32[]{:S(2)}) collective-permute-start(bf16[1040,256]{1,0:T(8,128)(2,1)S(1)} %get-tuple-element.40.refs_8_.refs_1_), channel_id=1, source_target_pairs={{0,2},{1,3},{2,0},{3,1},{4,6},{5,7},{6,4},{7,5},{8,10},{9,11},{10,... | collective-permute-start | bytes 1597448 | tf_op jit(solution)/shard_map/ppermute | solution.py:27
  48.9 3.3 %collective-permute-start.16 = (f32[2,2,8,256]{3,2,1,0:T(8,128)S(1)}, f32[2,2,8,256]{3,2,1,0:T(8,128)S(1)}, u32[]{:S(2)}, u32[]{:S(2)}) collective-permute-start(f32[2,2,8,256]{3,2,1,0:T(8,128)S(1)} %pad_maximum_fusion.4), channel_id=1, source_target_pairs={{0,8},{4,12},{8,0},{12,4},{16,24},{20,28},{24,16},{28,20},{1,9},{5... | collective-permute-start | bytes 98312 | tf_op jit(solution)/shard_map/ppermute | solution.py:329
  52.1 2.6 %collective-permute-start.17 = (f32[2,2,8,256]{3,2,1,0:T(8,128)S(1)}, f32[2,2,8,256]{3,2,1,0:T(8,128)S(1)}, u32[]{:S(2)}, u32[]{:S(2)}) collective-permute-start(f32[2,2,8,256]{3,2,1,0:T(8,128)S(1)} %pad_maximum_fusion.4), channel_id=1, source_target_pairs={{0,16},{4,20},{8,24},{12,28},{16,0},{20,4},{24,8},{28,12},{1,17},{... | collective-permute-start | bytes 98312 | tf_op jit(solution)/shard_map/ppermute | solution.py:329
  54.7 1.4 %conv_edge.1.refs_2_ = bf16[512,256]{1,0:T(8,128)(2,1)S(1)} custom-call(bf16[1024,256]{1,0:T(8,128)(2,1)S(1)} %get-tuple-element.34.refs_0_.refs_2_, bf16[512,256]{1,0:T(8,128)(2,1)S(1)} %collective-permute-done.7.refs_1_, bf16[512,256]{1,0:T(8,128)(2,1)S(1)} %collective-permute-done.10.refs_2_, ...), custom_call_target="tpu_custom_call" | custom-call | tf_op jit(solution)/shard_map/conv_edge/pallas_call | solution.py:440
  56.2 1.6 %collective-permute-start.21 = (bf16[512,256]{1,0:T(8,128)(2,1)S(1)}, bf16[512,256]{1,0:T(8,128)(2,1)}, u32[]{:S(2)}, u32[]{:S(2)}) collective-permute-start(bf16[512,256]{1,0:T(8,128)(2,1)S(1)} %conv_edge.1.refs_2_), channel_id=1, source_target_pairs={{0,2},{1,3},{2,0},{3,1},{4,6},{5,7},{6,4},{7,5},{8,10},{9,11},{10,... | collective-permute-start | bytes 786440 | tf_op jit(solution)/shard_map/ppermute | solution.py:27
  57.7 2.7 %collective-permute-done.18 = f32[2,2,8,256]{3,2,1,0:T(8,128)S(1)} collective-permute-done((f32[2,2,8,256]{3,2,1,0:T(8,128)S(1)}, f32[2,2,8,256]{3,2,1,0:T(8,128)S(1)}, u32[]{:S(2)}, u32[]{:S(2)}) %collective-permute-start.18) | collective-permute-done | bytes 32800 | tf_op jit(solution)/shard_map/ppermute | solution.py:329
  63.3 3.9 %collective-permute-done.21.refs_2_ = bf16[512,256]{1,0:T(8,128)(2,1)} collective-permute-done((bf16[512,256]{1,0:T(8,128)(2,1)S(1)}, bf16[512,256]{1,0:T(8,128)(2,1)}, u32[]{:S(2)}, u32[]{:S(2)}) %collective-permute-start.21) | collective-permute-done | bytes 262176 | tf_op jit(solution)/shard_map/ppermute | solution.py:27
  67.3 2.9 %fetch_two.1.refs_7_ = bf16[4,3,3,256,256]{4,3,2,1,0:T(8,128)(2,1)S(1)} custom-call(s32[4]{0:T(128)S(1)} %pad_add_fusion.1.refs_0_.src, bf16[3,3,1024,256]{3,2,1,0:T(8,128)(2,1)} %w.2), custom_call_target="tpu_custom_call" | custom-call | tf_op jit(solution)/shard_map/fetch_two/pallas_call | solution.py:455
  70.3 3.8 %two_near.1.refs_8_ = f32[3,4,256,256]{3,2,1,0:T(8,128)S(1)} custom-call(s32[2]{0:T(128)S(1)} %add_convert_fusion.1.refs_0_, bf16[1040,256]{1,0:T(8,128)(2,1)S(1)} %get-tuple-element.40.refs_8_.refs_1_, bf16[512,256]{1,0:T(8,128)(2,1)S(1)} %conv_edge.1.refs_2_, bf16[1040,256]{1,0:T(8,128)(2,1)} %collective-permute-done.14.refs_3_, ...), custom_call_target="tpu_custom_call" | custom-call | tf_op jit(solution)/shard_map/two_near/pallas_call | solution.py:464
  74.1 5.0 %two_far.1 = (f32[1024,256]{1,0:T(8,128)S(1)}, bf16[1040,256]{1,0:T(8,128)(2,1)S(1)}, f32[2,8,256]{2,1,0:T(8,128)S(1)}) custom-call(s32[2]{0:T(128)S(1)} %add_convert_fusion.1.refs_0_, bf16[1040,256]{1,0:T(8,128)(2,1)S(1)} %collective-permute-done.20.refs_1_, bf16[512,256]{1,0:T(8,128)(2,1)} %collective-permute-done.21.refs_2_, ...), custom_call_target="tpu_custom_call" | custom-call | tf_op jit(solution)/shard_map/two_far/pallas_call | solution.py:477
  79.1 1.7 %collective-permute-start.24 = (f32[2,8,256]{2,1,0:T(8,128)S(1)}, f32[2,8,256]{2,1,0:T(8,128)S(1)}, u32[]{:S(2)}, u32[]{:S(2)}) collective-permute-start(f32[2,8,256]{2,1,0:T(8,128)S(1)} %get-tuple-element.50), channel_id=1, source_target_pairs={{0,2},{1,3},{2,0},{3,1},{4,6},{5,7},{6,4},{7,5},{8,10},{9,11},{10,... | collective-permute-start | bytes 49160 | tf_op jit(solution)/shard_map/ppermute | solution.py:27
  80.9 2.0 %collective-permute-done.24 = f32[2,8,256]{2,1,0:T(8,128)S(1)} collective-permute-done((f32[2,8,256]{2,1,0:T(8,128)S(1)}, f32[2,8,256]{2,1,0:T(8,128)S(1)}, u32[]{:S(2)}, u32[]{:S(2)}) %collective-permute-start.24) | collective-permute-done | bytes 16416 | tf_op jit(solution)/shard_map/ppermute | solution.py:27
  83.0 3.8 %collective-permute-done.25 = f32[2,2,8,256]{3,2,1,0:T(8,128)S(1)} collective-permute-done((f32[2,2,8,256]{3,2,1,0:T(8,128)S(1)}, f32[2,2,8,256]{3,2,1,0:T(8,128)S(1)}, u32[]{:S(2)}, u32[]{:S(2)}) %collective-permute-start.25) | collective-permute-done | bytes 32800 | tf_op jit(solution)/shard_map/ppermute | solution.py:329
  86.8 1.9 %collective-permute-start.26 = (f32[2,2,8,256]{3,2,1,0:T(8,128)S(1)}, f32[2,2,8,256]{3,2,1,0:T(8,128)S(1)}, u32[]{:S(2)}, u32[]{:S(2)}) collective-permute-start(f32[2,2,8,256]{3,2,1,0:T(8,128)S(1)} %pad_maximum_fusion.5), channel_id=1, source_target_pairs={{0,8},{4,12},{8,0},{12,4},{16,24},{20,28},{24,16},{28,20},{1,9},{5... | collective-permute-start | bytes 98312 | tf_op jit(solution)/shard_map/ppermute | solution.py:329
  88.7 2.6 %collective-permute-start.27 = (f32[2,2,8,256]{3,2,1,0:T(8,128)S(1)}, f32[2,2,8,256]{3,2,1,0:T(8,128)S(1)}, u32[]{:S(2)}, u32[]{:S(2)}) collective-permute-start(f32[2,2,8,256]{3,2,1,0:T(8,128)S(1)} %pad_maximum_fusion.5), channel_id=1, source_target_pairs={{0,16},{4,20},{8,24},{12,28},{16,0},{20,4},{24,8},{28,12},{1,17},{... | collective-permute-start | bytes 98312 | tf_op jit(solution)/shard_map/ppermute | solution.py:329
  91.5 1.8 %collective-permute-start.30 = (bf16[1040,256]{1,0:T(8,128)(2,1)S(1)}, bf16[1040,256]{1,0:T(8,128)(2,1)S(1)}, u32[]{:S(2)}, u32[]{:S(2)}) collective-permute-start(bf16[1040,256]{1,0:T(8,128)(2,1)S(1)} %get-tuple-element.52.refs_4_), channel_id=1, source_target_pairs={{0,2},{1,3},{2,0},{3,1},{4,6},{5,7},{6,4},{7,5},{8,10},{9,11},{10,... | collective-permute-start | bytes 1597448 | tf_op jit(solution)/shard_map/ppermute | solution.py:27
  93.3 2.8 %fetch_head.1.refs_12_ = bf16[4,256,2048]{2,1,0:T(8,128)(2,1)S(1)} custom-call(s32[4]{0:T(128)S(1)} %pad_add_fusion.1.refs_0_.src, bf16[1024,2048]{1,0:T(8,128)(2,1)} %w.3), custom_call_target="tpu_custom_call" | custom-call | tf_op jit(solution)/shard_map/fetch_head/pallas_call | solution.py:493
  97.1 6.1 %collective-permute-done.30.refs_6_ = bf16[1040,256]{1,0:T(8,128)(2,1)S(1)} collective-permute-done((bf16[1040,256]{1,0:T(8,128)(2,1)S(1)}, bf16[1040,256]{1,0:T(8,128)(2,1)S(1)}, u32[]{:S(2)}, u32[]{:S(2)}) %collective-permute-start.30) | collective-permute-done | bytes 532512 | tf_op jit(solution)/shard_map/ppermute | solution.py:27
  105.2 5.6 %head.1 = f32[8,1024]{1,0:T(8,128)S(1)} custom-call(bf16[1024,256]{1,0:T(8,128)(2,1)S(1)} %get-tuple-element.101.refs_1_.refs_0_, bf16[1024,256]{1,0:T(8,128)(2,1)S(1)} %collective-permute-done.4.refs_4_.refs_1_, bf16[1024,256]{1,0:T(8,128)(2,1)S(1)} %get-tuple-element.34.refs_0_.refs_2_, bf16[1024,256]{1,0:T(8,128)(2,1)S(1)} %collective-permute-done.8.refs_2_.refs_3_, ...), custom_call_target="tpu_custom_call" | custom-call | tf_op jit(solution)/shard_map/head/pallas_call | solution.py:509
  112.7 1.5 %collective-permute-done.33 = f32[8,1024]{1,0:T(8,128)S(1)} collective-permute-done((f32[8,1024]{1,0:T(8,128)S(1)}, f32[8,1024]{1,0:T(8,128)S(1)}, u32[]{:S(2)}, u32[]{:S(2)}) %collective-permute-start.33) | collective-permute-done | bytes 32800 | tf_op jit(solution)/shard_map/ppermute | solution.py:525
  114.2 1.8 %collective-permute-done.34 = f32[8,1024]{1,0:T(8,128)S(1)} collective-permute-done((f32[8,1024]{1,0:T(8,128)S(1)}, f32[8,1024]{1,0:T(8,128)S(1)}, u32[]{:S(2)}, u32[]{:S(2)}) %collective-permute-start.34) | collective-permute-done | bytes 32800 | tf_op jit(solution)/shard_map/ppermute | solution.py:525
  (123 shorter events, 16.0 us)
Async XLA Ops:
  7.8 9.1 %collective-permute-start.3 = (s32[512]{0:T(512)S(1)}, s32[512]{0:T(512)S(1)}, u32[]{:S(2)}, u32[]{:S(2)}) collective-permute-start(s32[512]{0:T(512)S(1)} %get-tuple-element.94), channel_id=1, source_target_pairs={{4,0},{8,4},{12,8},{16,12},{20,16},{24,20},{28,24},{5,1},{9,5},{13... | collective-permute-start | bytes 6152 | tf_op jit(solution)/shard_map/ppermute | solution.py:66
  9.1 15.9 %collective-permute-start = (bf16[1024,256]{1,0:T(8,128)(2,1)S(1)}, bf16[1024,256]{1,0:T(8,128)(2,1)S(1)}, u32[]{:S(2)}, u32[]{:S(2)}) collective-permute-start(bf16[1024,256]{1,0:T(8,128)(2,1)S(1)} %gather_fusion), channel_id=1, source_target_pairs={{0,2},{1,3},{2,0},{3,1},{4,6},{5,7},{6,4},{7,5},{8,10},{9,11},{10,... | collective-permute-start | bytes 1572872 | tf_op jit(solution)/shard_map/ppermute | solution.py:27
  12.1 5.8 %collective-permute-start.2 = (s32[512]{0:T(512)S(1)}, s32[512]{0:T(512)S(1)}, u32[]{:S(2)}, u32[]{:S(2)}) collective-permute-start(s32[512]{0:T(512)S(1)} %get-tuple-element.93), channel_id=1, source_target_pairs={{0,4},{4,8},{8,12},{12,16},{16,20},{20,24},{24,28},{1,5},{5,9},{9,... | collective-permute-start | bytes 6152 | tf_op jit(solution)/shard_map/ppermute | solution.py:61
  16.7 8.2 %collective-permute-start.1 = (f32[5,8,256]{2,1,0:T(8,128)S(1)}, f32[5,8,256]{2,1,0:T(8,128)S(1)}, u32[]{:S(2)}, u32[]{:S(2)}) collective-permute-start(f32[5,8,256]{2,1,0:T(8,128)S(1)} %broadcast_in_dim.74), channel_id=1, source_target_pairs={{0,2},{1,3},{2,0},{3,1},{4,6},{5,7},{6,4},{7,5},{8,10},{9,11},{10,... | collective-permute-start | bytes 122888 | tf_op jit(solution)/shard_map/ppermute | solution.py:27
  26.0 2.7 %collective-permute-start.4 = (bf16[1024,256]{1,0:T(8,128)(2,1)S(1)}, bf16[1024,256]{1,0:T(8,128)(2,1)S(1)}, u32[]{:S(2)}, u32[]{:S(2)}) collective-permute-start(bf16[1024,256]{1,0:T(8,128)(2,1)S(1)} %get-tuple-element.101.refs_1_.refs_0_), channel_id=1, source_target_pairs={{0,1},{1,0},{2,3},{3,2},{4,5},{5,4},{6,7},{7,6},{8,9},{9,8},{10,11... | collective-permute-start | bytes 1572872 | tf_op jit(solution)/shard_map/ppermute | solution.py:21
  26.1 2.5 %collective-permute-start.5 = (bf16[512,256]{1,0:T(8,128)(2,1)S(1)}, bf16[512,256]{1,0:T(8,128)(2,1)S(1)}, u32[]{:S(2)}, u32[]{:S(2)}) collective-permute-start(bf16[512,256]{1,0:T(8,128)(2,1)S(1)} %get-tuple-element.78.refs_2_), channel_id=1, source_target_pairs={{0,1},{1,0},{2,3},{3,2},{4,5},{5,4},{6,7},{7,6},{8,9},{9,8},{10,11... | collective-permute-start | bytes 786440 | tf_op jit(solution)/shard_map/ppermute | solution.py:21
  26.8 8.6 %collective-permute-start.7 = (bf16[512,256]{1,0:T(8,128)(2,1)S(1)}, bf16[512,256]{1,0:T(8,128)(2,1)S(1)}, u32[]{:S(2)}, u32[]{:S(2)}) collective-permute-start(bf16[512,256]{1,0:T(8,128)(2,1)S(1)} %get-tuple-element.78.refs_2_), channel_id=1, source_target_pairs={{0,2},{1,3},{2,0},{3,1},{4,6},{5,7},{6,4},{7,5},{8,10},{9,11},{10,... | collective-permute-start | bytes 786440 | tf_op jit(solution)/shard_map/ppermute | solution.py:27
  34.8 2.4 %collective-permute-start.8 = (bf16[1024,256]{1,0:T(8,128)(2,1)S(1)}, bf16[1024,256]{1,0:T(8,128)(2,1)S(1)}, u32[]{:S(2)}, u32[]{:S(2)}) collective-permute-start(bf16[1024,256]{1,0:T(8,128)(2,1)S(1)} %get-tuple-element.34.refs_0_.refs_2_), channel_id=1, source_target_pairs={{0,1},{1,0},{2,3},{3,2},{4,5},{5,4},{6,7},{7,6},{8,9},{9,8},{10,11... | collective-permute-start | bytes 1572872 | tf_op jit(solution)/shard_map/ppermute | solution.py:21
  35.5 11.5 %collective-permute-start.10 = (bf16[512,256]{1,0:T(8,128)(2,1)S(1)}, bf16[512,256]{1,0:T(8,128)(2,1)S(1)}, u32[]{:S(2)}, u32[]{:S(2)}) collective-permute-start(bf16[512,256]{1,0:T(8,128)(2,1)S(1)} %get-tuple-element.77.refs_3_), channel_id=1, source_target_pairs={{0,2},{1,3},{2,0},{3,1},{4,6},{5,7},{6,4},{7,5},{8,10},{9,11},{10,... | collective-permute-start | bytes 786440 | tf_op jit(solution)/shard_map/ppermute | solution.py:27
  40.7 3.8 %collective-permute-start.12 = (f32[2,8,256]{2,1,0:T(8,128)S(1)}, f32[2,8,256]{2,1,0:T(8,128)S(1)}, u32[]{:S(2)}, u32[]{:S(2)}) collective-permute-start(f32[2,8,256]{2,1,0:T(8,128)S(1)} %get-tuple-element.39), channel_id=1, source_target_pairs={{0,2},{1,3},{2,0},{3,1},{4,6},{5,7},{6,4},{7,5},{8,10},{9,11},{10,... | collective-permute-start | bytes 49160 | tf_op jit(solution)/shard_map/ppermute | solution.py:27
  44.5 4.3 %collective-permute-start.13 = (f32[2,2,8,256]{3,2,1,0:T(8,128)S(1)}, f32[2,2,8,256]{3,2,1,0:T(8,128)S(1)}, u32[]{:S(2)}, u32[]{:S(2)}) collective-permute-start(f32[2,2,8,256]{3,2,1,0:T(8,128)S(1)} %pad_maximum_fusion), channel_id=1, source_target_pairs={{0,4},{4,0},{8,12},{12,8},{16,20},{20,16},{24,28},{28,24},{1,5},{5... | collective-permute-start | bytes 98312 | tf_op jit(solution)/shard_map/ppermute | solution.py:329
  46.9 7.8 %collective-permute-start.11 = (bf16[512,256]{1,0:T(8,128)(2,1)S(1)}, bf16[512,256]{1,0:T(8,128)(2,1)S(1)}, u32[]{:S(2)}, u32[]{:S(2)}) collective-permute-start(bf16[512,256]{1,0:T(8,128)(2,1)S(1)} %collective-permute-done.10.refs_2_), channel_id=1, source_target_pairs={{0,1},{1,0},{2,3},{3,2},{4,5},{5,4},{6,7},{7,6},{8,9},{9,8},{10,11... | collective-permute-start | bytes 786440 | tf_op jit(solution)/shard_map/ppermute | solution.py:21
  46.9 15.0 %collective-permute-start.20 = (bf16[1040,256]{1,0:T(8,128)(2,1)S(1)}, bf16[1040,256]{1,0:T(8,128)(2,1)S(1)}, u32[]{:S(2)}, u32[]{:S(2)}) collective-permute-start(bf16[1040,256]{1,0:T(8,128)(2,1)S(1)} %get-tuple-element.40.refs_8_.refs_1_), channel_id=1, source_target_pairs={{0,2},{1,3},{2,0},{3,1},{4,6},{5,7},{6,4},{7,5},{8,10},{9,11},{10,... | collective-permute-start | bytes 1597448 | tf_op jit(solution)/shard_map/ppermute | solution.py:27
  48.9 7.3 %collective-permute-start.16 = (f32[2,2,8,256]{3,2,1,0:T(8,128)S(1)}, f32[2,2,8,256]{3,2,1,0:T(8,128)S(1)}, u32[]{:S(2)}, u32[]{:S(2)}) collective-permute-start(f32[2,2,8,256]{3,2,1,0:T(8,128)S(1)} %pad_maximum_fusion.4), channel_id=1, source_target_pairs={{0,8},{4,12},{8,0},{12,4},{16,24},{20,28},{24,16},{28,20},{1,9},{5... | collective-permute-start | bytes 98312 | tf_op jit(solution)/shard_map/ppermute | solution.py:329
  52.1 5.6 %collective-permute-start.17 = (f32[2,2,8,256]{3,2,1,0:T(8,128)S(1)}, f32[2,2,8,256]{3,2,1,0:T(8,128)S(1)}, u32[]{:S(2)}, u32[]{:S(2)}) collective-permute-start(f32[2,2,8,256]{3,2,1,0:T(8,128)S(1)} %pad_maximum_fusion.4), channel_id=1, source_target_pairs={{0,16},{4,20},{8,24},{12,28},{16,0},{20,4},{24,8},{28,12},{1,17},{... | collective-permute-start | bytes 98312 | tf_op jit(solution)/shard_map/ppermute | solution.py:329
  54.7 5.7 %collective-permute-start.18 = (f32[2,2,8,256]{3,2,1,0:T(8,128)S(1)}, f32[2,2,8,256]{3,2,1,0:T(8,128)S(1)}, u32[]{:S(2)}, u32[]{:S(2)}) collective-permute-start(f32[2,2,8,256]{3,2,1,0:T(8,128)S(1)} %pad_maximum_fusion.4), channel_id=1, source_target_pairs={{0,24},{4,28},{8,16},{12,20},{16,8},{20,12},{24,0},{28,4},{1,25},{... | collective-permute-start | bytes 98312 | tf_op jit(solution)/shard_map/ppermute | solution.py:329
  54.7 15.5 %collective-permute-start.14 = (bf16[1040,256]{1,0:T(8,128)(2,1)S(1)}, bf16[1040,256]{1,0:T(8,128)(2,1)}, u32[]{:S(2)}, u32[]{:S(2)}) collective-permute-start(bf16[1040,256]{1,0:T(8,128)(2,1)S(1)} %get-tuple-element.40.refs_8_.refs_1_), channel_id=1, source_target_pairs={{0,1},{1,0},{2,3},{3,2},{4,5},{5,4},{6,7},{7,6},{8,9},{9,8},{10,11... | collective-permute-start | bytes 1597448 | tf_op jit(solution)/shard_map/ppermute | solution.py:21
  56.2 11.0 %collective-permute-start.21 = (bf16[512,256]{1,0:T(8,128)(2,1)S(1)}, bf16[512,256]{1,0:T(8,128)(2,1)}, u32[]{:S(2)}, u32[]{:S(2)}) collective-permute-start(bf16[512,256]{1,0:T(8,128)(2,1)S(1)} %conv_edge.1.refs_2_), channel_id=1, source_target_pairs={{0,2},{1,3},{2,0},{3,1},{4,6},{5,7},{6,4},{7,5},{8,10},{9,11},{10,... | collective-permute-start | bytes 786440 | tf_op jit(solution)/shard_map/ppermute | solution.py:27
  61.9 12.2 %collective-permute-start.22 = (bf16[1040,256]{1,0:T(8,128)(2,1)S(1)}, bf16[1040,256]{1,0:T(8,128)(2,1)}, u32[]{:S(2)}, u32[]{:S(2)}) collective-permute-start(bf16[1040,256]{1,0:T(8,128)(2,1)S(1)} %collective-permute-done.20.refs_1_), channel_id=1, source_target_pairs={{0,1},{1,0},{2,3},{3,2},{4,5},{5,4},{6,7},{7,6},{8,9},{9,8},{10,11... | collective-permute-start | bytes 1597448 | tf_op jit(solution)/shard_map/ppermute | solution.py:21
  61.9 8.3 %collective-permute-start.15 = (bf16[512,256]{1,0:T(8,128)(2,1)S(1)}, bf16[512,256]{1,0:T(8,128)(2,1)S(1)}, u32[]{:S(2)}, u32[]{:S(2)}) collective-permute-start(bf16[512,256]{1,0:T(8,128)(2,1)S(1)} %conv_edge.1.refs_2_), channel_id=1, source_target_pairs={{0,1},{1,0},{2,3},{3,2},{4,5},{5,4},{6,7},{7,6},{8,9},{9,8},{10,11... | collective-permute-start | bytes 786440 | tf_op jit(solution)/shard_map/ppermute | solution.py:21
  63.2 7.0 %collective-permute-start.19 = (f32[2,2,8,256]{3,2,1,0:T(8,128)S(1)}, f32[2,2,8,256]{3,2,1,0:T(8,128)S(1)}, u32[]{:S(2)}, u32[]{:S(2)}) collective-permute-start(f32[2,2,8,256]{3,2,1,0:T(8,128)S(1)} %pad_maximum_fusion.1), channel_id=1, source_target_pairs={{0,1},{1,0},{2,3},{3,2},{4,5},{5,4},{6,7},{7,6},{8,9},{9,8},{10,11... | collective-permute-start | bytes 98312 | tf_op jit(solution)/shard_map/ppermute | solution.py:21
  67.2 6.9 %collective-permute-start.23 = (bf16[512,256]{1,0:T(8,128)(2,1)}, bf16[512,256]{1,0:T(8,128)(2,1)S(1)}, u32[]{:S(2)}, u32[]{:S(2)}) collective-permute-start(bf16[512,256]{1,0:T(8,128)(2,1)} %collective-permute-done.21.refs_2_), channel_id=1, source_target_pairs={{0,1},{1,0},{2,3},{3,2},{4,5},{5,4},{6,7},{7,6},{8,9},{9,8},{10,11... | collective-permute-start | bytes 786440 | tf_op jit(solution)/shard_map/ppermute | solution.py:21
  79.1 3.8 %collective-permute-start.24 = (f32[2,8,256]{2,1,0:T(8,128)S(1)}, f32[2,8,256]{2,1,0:T(8,128)S(1)}, u32[]{:S(2)}, u32[]{:S(2)}) collective-permute-start(f32[2,8,256]{2,1,0:T(8,128)S(1)} %get-tuple-element.50), channel_id=1, source_target_pairs={{0,2},{1,3},{2,0},{3,1},{4,6},{5,7},{6,4},{7,5},{8,10},{9,11},{10,... | collective-permute-start | bytes 49160 | tf_op jit(solution)/shard_map/ppermute | solution.py:27
  82.9 3.9 %collective-permute-start.25 = (f32[2,2,8,256]{3,2,1,0:T(8,128)S(1)}, f32[2,2,8,256]{3,2,1,0:T(8,128)S(1)}, u32[]{:S(2)}, u32[]{:S(2)}) collective-permute-start(f32[2,2,8,256]{3,2,1,0:T(8,128)S(1)} %pad_maximum_fusion.2), channel_id=1, source_target_pairs={{0,4},{4,0},{8,12},{12,8},{16,20},{20,16},{24,28},{28,24},{1,5},{5... | collective-permute-start | bytes 98312 | tf_op jit(solution)/shard_map/ppermute | solution.py:329
  86.8 9.2 %collective-permute-start.26 = (f32[2,2,8,256]{3,2,1,0:T(8,128)S(1)}, f32[2,2,8,256]{3,2,1,0:T(8,128)S(1)}, u32[]{:S(2)}, u32[]{:S(2)}) collective-permute-start(f32[2,2,8,256]{3,2,1,0:T(8,128)S(1)} %pad_maximum_fusion.5), channel_id=1, source_target_pairs={{0,8},{4,12},{8,0},{12,4},{16,24},{20,28},{24,16},{28,20},{1,9},{5... | collective-permute-start | bytes 98312 | tf_op jit(solution)/shard_map/ppermute | solution.py:329
  88.7 7.4 %collective-permute-start.27 = (f32[2,2,8,256]{3,2,1,0:T(8,128)S(1)}, f32[2,2,8,256]{3,2,1,0:T(8,128)S(1)}, u32[]{:S(2)}, u32[]{:S(2)}) collective-permute-start(f32[2,2,8,256]{3,2,1,0:T(8,128)S(1)} %pad_maximum_fusion.5), channel_id=1, source_target_pairs={{0,16},{4,20},{8,24},{12,28},{16,0},{20,4},{24,8},{28,12},{1,17},{... | collective-permute-start | bytes 98312 | tf_op jit(solution)/shard_map/ppermute | solution.py:329
  91.3 5.7 %collective-permute-start.28 = (f32[2,2,8,256]{3,2,1,0:T(8,128)S(1)}, f32[2,2,8,256]{3,2,1,0:T(8,128)S(1)}, u32[]{:S(2)}, u32[]{:S(2)}) collective-permute-start(f32[2,2,8,256]{3,2,1,0:T(8,128)S(1)} %pad_maximum_fusion.5), channel_id=1, source_target_pairs={{0,24},{4,28},{8,16},{12,20},{16,8},{20,12},{24,0},{28,4},{1,25},{... | collective-permute-start | bytes 98312 | tf_op jit(solution)/shard_map/ppermute | solution.py:329
  91.5 11.7 %collective-permute-start.30 = (bf16[1040,256]{1,0:T(8,128)(2,1)S(1)}, bf16[1040,256]{1,0:T(8,128)(2,1)S(1)}, u32[]{:S(2)}, u32[]{:S(2)}) collective-permute-start(bf16[1040,256]{1,0:T(8,128)(2,1)S(1)} %get-tuple-element.52.refs_4_), channel_id=1, source_target_pairs={{0,2},{1,3},{2,0},{3,1},{4,6},{5,7},{6,4},{7,5},{8,10},{9,11},{10,... | collective-permute-start | bytes 1597448 | tf_op jit(solution)/shard_map/ppermute | solution.py:27
  93.3 11.9 %collective-permute-start.29 = (bf16[1040,256]{1,0:T(8,128)(2,1)S(1)}, bf16[1040,256]{1,0:T(8,128)(2,1)S(1)}, u32[]{:S(2)}, u32[]{:S(2)}) collective-permute-start(bf16[1040,256]{1,0:T(8,128)(2,1)S(1)} %get-tuple-element.52.refs_4_), channel_id=1, source_target_pairs={{0,1},{1,0},{2,3},{3,2},{4,5},{5,4},{6,7},{7,6},{8,9},{9,8},{10,11... | collective-permute-start | bytes 1597448 | tf_op jit(solution)/shard_map/ppermute | solution.py:21
  110.8 3.4 %collective-permute-start.33 = (f32[8,1024]{1,0:T(8,128)S(1)}, f32[8,1024]{1,0:T(8,128)S(1)}, u32[]{:S(2)}, u32[]{:S(2)}) collective-permute-start(f32[8,1024]{1,0:T(8,128)S(1)} %head.1), channel_id=1, source_target_pairs={{0,3},{1,2},{2,1},{3,0},{4,7},{5,6},{6,5},{7,4},{8,11},{9,10},{10,... | collective-permute-start | bytes 98312 | tf_op jit(solution)/shard_map/ppermute | solution.py:525
  112.1 3.9 %collective-permute-start.34 = (f32[8,1024]{1,0:T(8,128)S(1)}, f32[8,1024]{1,0:T(8,128)S(1)}, u32[]{:S(2)}, u32[]{:S(2)}) collective-permute-start(f32[8,1024]{1,0:T(8,128)S(1)} %head.1), channel_id=1, source_target_pairs={{0,2},{1,3},{2,0},{3,1},{4,6},{5,7},{6,4},{7,5},{8,10},{9,11},{10,... | collective-permute-start | bytes 98312 | tf_op jit(solution)/shard_map/ppermute | solution.py:525
  112.6 3.4 %collective-permute-start.35 = (f32[8,1024]{1,0:T(8,128)S(1)}, f32[8,1024]{1,0:T(8,128)S(1)}, u32[]{:S(2)}, u32[]{:S(2)}) collective-permute-start(f32[8,1024]{1,0:T(8,128)S(1)} %head.1), channel_id=1, source_target_pairs={{0,1},{1,0},{2,3},{3,2},{4,5},{5,4},{6,7},{7,6},{8,9},{9,8},{10,11... | collective-permute-start | bytes 98312 | tf_op jit(solution)/shard_map/ppermute | solution.py:525
  (14 other events, 111.7 us)
